TPU v7x, 32 devices: a whole 2x2x4 slice. The times are simulated.
32 devices in a mesh: groups: 2 (over y), wide: 4 (over z), narrow: 4 (over x, core).
Axes of the slice: x: 2, y: 2, z: 4, core: 2. Of those that a mesh axis runs over, the one named last changes fastest.
Arguments:
- tokens: bfloat16 [512, 4096], P(('groups', 'wide'), 'narrow'), parts along dimension 0, may hold values from -6 to 6
- routes: int32 [512, 8], P(('groups', 'wide')), parts along dimension 0, may hold values from 0 to 15, all different within a row; in each aligned block of 64 rows (0 to 63, 64 to 127, ...) at most 40 rows name the same one
- gate_weights: float32 [512, 8], P(('groups', 'wide')), parts along dimension 0, may hold values from 0.05 to 1
- delta_of: int32 [16], replicated, may hold values from 0 to 15, each once
- base_gate: bfloat16 [4096, 1536], P('wide', 'narrow'), may hold values from -0.09375 to 0.09375
- base_up: bfloat16 [4096, 1536], P('wide', 'narrow'), may hold values from -0.09375 to 0.09375
- base_down: bfloat16 [1536, 4096], P('wide', 'narrow'), may hold values from -0.15625 to 0.15625
- gate_left: bfloat16 [16, 4096, 32], P('wide', 'narrow'), may hold values from -0.09375 to 0.09375
- gate_right: bfloat16 [16, 32, 1536], P('wide', None, 'narrow'), may hold values from -0.5 to 0.5
- up_left: bfloat16 [16, 4096, 32], P('wide', 'narrow'), may hold values from -0.09375 to 0.09375
- up_right: bfloat16 [16, 32, 1536], P('wide', None, 'narrow'), may hold values from -0.5 to 0.5
- down_left: bfloat16 [16, 1536, 32], P('wide', 'narrow'), may hold values from -0.15625 to 0.15625
- down_right: bfloat16 [16, 32, 4096], P('wide', None, 'narrow'), may hold values from -0.5 to 0.5
Outputs:
- mixed_out: bfloat16 [512, 4096], P(('groups', 'wide'), 'narrow'), parts along dimension 0
There are 2 independent parts, one for each index of `groups`. A program takes and returns all parts, laid end to end along the dimension named above; an argument that names none is the same for every part. Nothing has to cross between parts.
Inputs may be any that keep to these rules, and one draw needn't show every extreme that they name: `routes`: in each aligned block of 64 rows (the rows of one index of wide) no expert is named by more than 40 rows, and in some block some expert is named by exactly 40 rows.
All inputs are finite; a program needn't handle non-finite values.
Results may differ from a plain program's by a relative error of at most 0.0053.
Values may be sent and summed in bfloat16 or wider, within the bound.
A program may use at most 64 MiB of HBM per device.

v0:
```python
import jax
import jax.numpy as jnp
from jax import lax
from jax.sharding import PartitionSpec as P


def with_zero_row(rows):
    return jnp.concatenate([rows, jnp.zeros((1, rows.shape[1]), rows.dtype)], axis=0)


def rebuild(base_rows, left_rows, right_factor):
    product = jnp.einsum(
        "ecr,erf->ecf", left_rows, right_factor, preferred_element_type=jnp.float32
    )
    return (base_rows.astype(jnp.float32)[None] + product).astype(jnp.bfloat16)


def shards(
    tokens,
    routes,
    gate_weights,
    delta_of,
    base_gate,
    base_up,
    base_down,
    gate_left,
    gate_right,
    up_left,
    up_right,
    down_left,
    down_right,
):
    block_rows, top_count = routes.shape
    feature_part = tokens.shape[1]
    exp_here = gate_left.shape[0]
    wide_count = lax.axis_size("wide")
    experts = wide_count * exp_here
    capacity = max(2, block_rows * top_count * 5 // (4 * experts))
    slot_total = experts * capacity
    expert_ids = lax.broadcasted_iota(jnp.int32, (1, 1, experts), 2)
    onehot = (routes[:, :, None] == expert_ids).astype(jnp.float32)
    routed = jnp.sum(onehot, axis=1)
    row_index = lax.broadcasted_iota(jnp.int32, (block_rows, block_rows), 0)
    col_index = lax.broadcasted_iota(jnp.int32, (block_rows, block_rows), 1)
    earlier_mask = (col_index < row_index).astype(jnp.float32)
    before = jnp.dot(
        earlier_mask, routed, preferred_element_type=jnp.float32, precision=lax.Precision.HIGHEST
    )
    place_in = jnp.sum(onehot * before[:, None, :], axis=2).astype(jnp.int32)
    delta_ids = jnp.sum(onehot * delta_of.astype(jnp.float32)[None, None, :], axis=2).astype(
        jnp.int32
    )
    position = delta_ids * capacity + place_in
    every_row = lax.all_gather(tokens, "wide", axis=0, tiled=True)
    every_place = lax.all_gather(position, "wide", axis=0, tiled=True)
    own_first = lax.axis_index("wide") * (exp_here * capacity)
    local_place = every_place - own_first
    owned = (local_place >= 0) & (local_place < exp_here * capacity)
    block_ids = lax.broadcasted_iota(jnp.int32, every_place.shape, 0) // block_rows
    target = jnp.where(owned, block_ids * (exp_here * capacity) + local_place, slot_total)
    every_token = lax.broadcasted_iota(jnp.int32, every_place.shape, 0)
    picked_rows = (
        jnp.full((slot_total,), every_row.shape[0], jnp.int32)
        .at[target.reshape(-1)]
        .set(every_token.reshape(-1), mode="drop")
    )
    local_rows = jnp.take(with_zero_row(every_row), picked_rows, axis=0).reshape(
        wide_count, exp_here, capacity, feature_part
    )
    slot_rows = lax.all_gather(local_rows, "narrow", axis=3, tiled=True)
    left_gate, left_up, left_down = (
        lax.all_gather(gate_left, "narrow", axis=1, tiled=True),
        lax.all_gather(up_left, "narrow", axis=1, tiled=True),
        lax.all_gather(down_left, "narrow", axis=1, tiled=True),
    )
    base_rows_gate = lax.all_gather(base_gate, "wide", axis=0, tiled=True)
    base_rows_up = lax.all_gather(base_up, "wide", axis=0, tiled=True)
    columns = slot_rows
    dense_gate = rebuild(base_rows_gate, left_gate, gate_right)
    dense_up = rebuild(base_rows_up, left_up, up_right)
    gate_sum = jnp.einsum("secd,edf->secf", columns, dense_gate, preferred_element_type=jnp.float32)
    up_sum = jnp.einsum("secd,edf->secf", columns, dense_up, preferred_element_type=jnp.float32)
    hidden = (jax.nn.silu(gate_sum) * up_sum).astype(jnp.bfloat16)
    hidden_all = lax.all_gather(hidden, "narrow", axis=3, tiled=True)
    dense_down = rebuild(
        lax.all_gather(base_down, "wide", axis=0, tiled=True), left_down, down_right
    )
    columns = hidden_all
    expert_out = jnp.einsum(
        "secf,efd->secd", columns, dense_down, preferred_element_type=jnp.float32
    ).astype(jnp.bfloat16)
    returned = lax.all_to_all(expert_out, "wide", split_axis=0, concat_axis=0, tiled=True).reshape(
        slot_total, feature_part
    )
    picked = jnp.take(returned, position.reshape(-1), axis=0).reshape(
        block_rows, top_count, feature_part
    )
    mixed_out = jnp.sum(gate_weights[:, :, None] * picked.astype(jnp.float32), axis=1)
    return mixed_out.astype(jnp.bfloat16)


def solution(mesh):
    return jax.shard_map(
        shards,
        mesh=mesh,
        in_specs=(
            P(("groups", "wide"), "narrow"),
            P(("groups", "wide"), None),
            P(("groups", "wide"), None),
            P(),
            P("wide", "narrow"),
            P("wide", "narrow"),
            P("wide", "narrow"),
            P("wide", "narrow", None),
            P("wide", None, "narrow"),
            P("wide", "narrow", None),
            P("wide", None, "narrow"),
            P("wide", "narrow", None),
            P("wide", None, "narrow"),
        ),
        out_specs=P(("groups", "wide"), "narrow"),
        check_vma=False,
    )
```

profile of v0, /device:TPU:0, one launch (start us, length us, event | category | flops | bytes accessed | tf_op | source)
XLA Modules:
  0.0 367.8 jit_solution(3245689724304477766)
XLA Ops:
  6.5 0.0 copy-start
  6.5 0.0 all-gather.11.cloned.1.call-start
  6.5 0.7 all-gather.11.cloned.1.call-update
  7.3 0.0 all-gather.17.cloned.1.call-start
  7.3 0.7 all-gather.17.cloned.1.call-update
  8.0 0.0 all-gather.13.cloned.1.call-start
  8.1 0.7 all-gather.13.cloned.1.call-update
  8.7 0.0 all-gather.15.cloned.1.call-start
  8.8 0.7 convert_reduce_fusion
  9.5 0.1 fusion.32
  9.6 0.7 convert_element_type.70
  10.3 0.8 select_reduce_fusion.1
  11.1 15.0 %all-gather = s32[4,64,8]{1,2,0:T(8,128)S(1)} all-gather(s32[1,64,8]{1,2,0:T(8,128)S(1)} %bitcast.60), channel_id=1, replica_groups=mesh['groups'=2,'wide'=4,'narrow'=4] {'wide'}, dimensions={0}, use_global_device_ids=true | all-gather | bytes 10240 | tf_op jit(solution)/shard_map/all_gather | solution.py:55
  26.2 0.1 reshape.144
  26.3 0.1 copy.44
  26.4 0.1 reshape.113
  26.6 0.1 reshape.136
  26.7 8.0 %scatter_custom_fusion = s32[640]{0:T(1024)S(1)} fusion(s32[2048]{0:T(1024)S(1)} %bitcast.62, s32[2048]{0:T(1024)S(1)} %reshape.136, s32[]{:T(128)} %constant.61.clone.1), kind=kCustom, calls=%fused_computation.45 | custom fusion | bytes 2564 | tf_op jit(solution)/shard_map/scatter | solution.py:65
  34.8 0.1 broadcast_in_dim.43
  34.9 23.1 %all_gather.35 = bf16[256,1024]{1,0:T(8,128)(2,1)S(1)} all-gather(bf16[64,1024]{1,0:T(8,128)(2,1)} %param.13), channel_id=1, replica_groups=mesh['groups'=2,'wide'=4,'narrow'=4] {'wide'}, dimensions={0}, use_global_device_ids=true | all-gather | bytes 655360 | tf_op jit(solution)/shard_map/all_gather | solution.py:54
  58.0 2.8 gather_fusion
  60.9 1.4 copy_select_fusion
  62.3 0.0 all-gather.15.cloned.1.call-update
  62.3 0.0 all-gather.19.cloned.1.call-start
  62.3 0.5 all-gather.19.cloned.1.call-update
  62.9 0.0 all-gather.9.cloned.1.call-start
  62.9 0.5 all-gather.9.cloned.1.call-update
  63.4 0.0 all-gather.21.cloned.1.call-start
  63.5 20.0 %all-gather.11.cloned.1.call-done = bf16[4096,384]{1,0:T(8,128)(2,1)} async-done(((bf16[1024,384]{1,0:T(8,128)(2,1)}), bf16[4096,384]{1,0:T(8,128)(2,1)}) %all-gather.11.cloned.1.call-update) | async-done | bytes 3145744 | tf_op jit(solution)/shard_map/all_gather | solution.py:76
  83.5 4.9 %convert_element_type.76 = f32[4096,384]{1,0:T(8,128)} convert(bf16[4096,384]{1,0:T(8,128)(2,1)} %all-gather.11.cloned.1.call-done) | non-fusion elementwise | flops 1572864 | bytes 9437184 | tf_op jit(solution)/shard_map/convert_element_type | solution.py:15
  88.4 0.0 copy-start.3
  88.4 58.7 %all-gather.17.cloned.1.call-done = bf16[4096,384]{1,0:T(8,128)(2,1)} async-done(((bf16[1024,384]{1,0:T(8,128)(2,1)}), bf16[4096,384]{1,0:T(8,128)(2,1)}) %all-gather.17.cloned.1.call-update) | async-done | bytes 3145744 | tf_op jit(solution)/shard_map/all_gather | solution.py:77
  147.1 5.0 %convert_element_type.78 = f32[4096,384]{1,0:T(8,128)} convert(bf16[4096,384]{1,0:T(8,128)(2,1)} %all-gather.17.cloned.1.call-done) | non-fusion elementwise | flops 1572864 | bytes 9437184 | tf_op jit(solution)/shard_map/convert_element_type | solution.py:15
  152.0 0.0 copy-start.4
  152.0 12.0 %all-gather.13.cloned.1.call-done = bf16[4,4096,32]{1,2,0:T(8,128)(2,1)} async-done(((bf16[4,1024,32]{1,2,0:T(8,128)(2,1)}), bf16[4,4096,32]{1,2,0:T(8,128)(2,1)}) %all-gather.13.cloned.1.call-update) | async-done | bytes 1048592 | tf_op jit(solution)/shard_map/all_gather | solution.py:72
  164.0 41.9 %all-gather.15.cloned.1.call-done = bf16[4,4,40,4096]{3,2,0,1:T(8,128)(2,1)} async-done(((bf16[4,4,40,1024]{3,2,0,1:T(8,128)(2,1)}), bf16[4,4,40,4096]{3,2,0,1:T(8,128)(2,1)}) %all-gather.15.cloned.1.call-update) | async-done | bytes 5242896 | tf_op jit(solution)/shard_map/all_gather | solution.py:70
  205.9 0.0 copy-done.3
  205.9 10.2 %fusion.23 = f32[4,4,40,384]{3,2,0,1:T(8,128)S(1)} fusion(bf16[4,4,40,4096]{3,2,0,1:T(8,128)(2,1)} %all-gather.15.cloned.1.call-done, f32[4096,384]{1,0:T(8,128)} %convert_element_type.76, bf16[4,4096,32]{1,2,0:T(8,128)(2,1)} %all-gather.13.cloned.1.call-done, bf16[4,32,384]{2,1,0:T(8,128)(2,1)S(1)} %copy-done.3), kind=kOutput, calls=%fused_computation.20 | convolution fusion | flops 2428502016 | bytes 13664256 | tf_op jit(solution)/shard_map/secd,edf->secf/dot_general | solution.py:81
  216.1 0.0 copy-start.1
  216.1 7.9 %all-gather.19.cloned.1.call-done = bf16[4,4096,32]{1,2,0:T(8,128)(2,1)} async-done(((bf16[4,1024,32]{1,2,0:T(8,128)(2,1)}), bf16[4,4096,32]{1,2,0:T(8,128)(2,1)}) %all-gather.19.cloned.1.call-update) | async-done | bytes 1048592 | tf_op jit(solution)/shard_map/all_gather | solution.py:73
  224.0 0.0 copy-done.4
  224.0 10.9 %fusion.29 = bf16[4,4,40,384]{3,2,0,1:T(8,128)(2,1)} fusion(bf16[4,4,40,4096]{3,2,0,1:T(8,128)(2,1)} %all-gather.15.cloned.1.call-done, f32[4096,384]{1,0:T(8,128)} %convert_element_type.78, bf16[4,4096,32]{1,2,0:T(8,128)(2,1)} %all-gather.19.cloned.1.call-done, bf16[4,32,384]{2,1,0:T(8,128)(2,1)S(1)} %copy-done.4, f32[4,4,40,384]{3,2,0,1:T(8,128)S(1)} %fusion.23), kind=kOutput, calls=%fused_computation.23 | convolution fusion | flops 2429976576 | bytes 14155776 | tf_op jit(solution)/shard_map/secd,edf->secf/dot_general | solution.py:82
  234.9 0.0 all-gather.21.cloned.1.call-update
  235.0 0.0 copy-done.1
  235.0 6.6 %all_gather.31 = bf16[4,1536,32]{1,2,0:T(8,128)(2,1)S(1)} all-gather(bf16[4,384,32]{1,2,0:T(8,128)(2,1)S(1)} %copy-done.1), channel_id=1, replica_groups=mesh['groups'=2,'wide'=4,'narrow'=4] {'narrow'}, dimensions={1}, use_global_device_ids=true | all-gather | bytes 491520 | tf_op jit(solution)/shard_map/all_gather | solution.py:74
  241.6 47.3 %all-gather.9.cloned.1.call-done = bf16[1536,1024]{1,0:T(8,128)(2,1)} async-done(((bf16[384,1024]{1,0:T(8,128)(2,1)}), bf16[1536,1024]{1,0:T(8,128)(2,1)}) %all-gather.9.cloned.1.call-update) | async-done | bytes 3145744 | tf_op jit(solution)/shard_map/all_gather | solution.py:86
  288.9 5.3 %convert_element_type.74 = f32[1536,1024]{1,0:T(8,128)} convert(bf16[1536,1024]{1,0:T(8,128)(2,1)} %all-gather.9.cloned.1.call-done) | non-fusion elementwise | flops 1572864 | bytes 9437184 | tf_op jit(solution)/shard_map/convert_element_type | solution.py:15
  294.2 16.7 %all-gather.21.cloned.1.call-done = bf16[4,4,40,1536]{3,2,0,1:T(8,128)(2,1)} async-done(((bf16[4,4,40,384]{3,2,0,1:T(8,128)(2,1)}), bf16[4,4,40,1536]{3,2,0,1:T(8,128)(2,1)}) %all-gather.21.cloned.1.call-update) | async-done | bytes 1966096 | tf_op jit(solution)/shard_map/all_gather | solution.py:84
  311.0 0.0 copy-done
  311.0 8.9 %fusion.17 = bf16[4,4,40,1024]{3,2,0,1:T(8,128)(2,1)S(1)} fusion(bf16[4,4,40,1536]{3,2,0,1:T(8,128)(2,1)} %all-gather.21.cloned.1.call-done, bf16[4,1536,32]{1,2,0:T(8,128)(2,1)S(1)} %all_gather.31, bf16[4,32,1024]{2,1,0:T(8,128)(2,1)S(1)} %copy-done, f32[1536,1024]{1,0:T(8,128)} %convert_element_type.74), kind=kOutput, calls=%fused_computation.18 | convolution fusion | flops 2429157376 | bytes 10223616 | tf_op jit(solution)/shard_map/secf,efd->secd/dot_general | solution.py:89
  319.8 0.0 copy-start.2
  319.8 1.2 copy.47
  321.1 4.6 %all-to-all-start = ((bf16[4,4,40,1024]{3,2,1,0:T(8,128)(2,1)}), bf16[4,4,40,1024]{3,2,1,0:T(8,128)(2,1)S(1)}, u32[]{:S(2)}, u32[]{:S(2)}) async-start(bf16[4,4,40,1024]{3,2,1,0:T(8,128)(2,1)} %copy.47), calls=%async_computation | async-start | bytes 2621440 | tf_op jit(solution)/shard_map/all_to_all | solution.py:92
  325.6 0.1 copy.48
  325.7 0.1 add.110
  325.8 0.1 copy.42
  325.9 0.0 copy-done.2
  325.9 0.1 copy.41
  326.0 31.4 %all-to-all-done = bf16[4,4,40,1024]{3,2,1,0:T(8,128)(2,1)S(1)} async-done(((bf16[4,4,40,1024]{3,2,1,0:T(8,128)(2,1)}), bf16[4,4,40,1024]{3,2,1,0:T(8,128)(2,1)S(1)}, u32[]{:S(2)}, u32[]{:S(2)}) %all-to-all-start) | async-done | bytes 1310752 | tf_op jit(solution)/shard_map/all_to_all | solution.py:92
  357.4 2.0 gather_fusion.1
  359.4 1.5 multiply_reduce_fusion
  (15 shorter events, 0.1 us)
Async XLA Ops:
  6.5 304.4 %copy-start = (bf16[4,32,1024]{2,1,0:T(8,128)(2,1)S(1)}, bf16[4,32,1024]{2,1,0:T(8,128)(2,1)}, u32[]{:S(2)}) copy-start(bf16[4,32,1024]{2,1,0:T(8,128)(2,1)} %param.25) | copy-start | bytes 786436
  6.5 76.9 %all-gather.11.cloned.1.call-start = ((), (), s32[]{:S(2)}) async-start(), calls=%async_computation.2 | async-start | bytes 3932160 | tf_op jit(solution)/shard_map/all_gather | solution.py:76
  7.3 139.8 %all-gather.17.cloned.1.call-start = ((), (), s32[]{:S(2)}) async-start(), calls=%async_computation.5 | async-start | bytes 3932160 | tf_op jit(solution)/shard_map/all_gather | solution.py:77
  8.0 156.0 %all-gather.13.cloned.1.call-start = ((), (), s32[]{:S(2)}) async-start(), calls=%async_computation.3 | async-start | bytes 1310720 | tf_op jit(solution)/shard_map/all_gather | solution.py:72
  8.7 197.1 %all-gather.15.cloned.1.call-start = ((), (), s32[]{:S(2)}) async-start(), calls=%async_computation.4 | async-start | bytes 6553600 | tf_op jit(solution)/shard_map/all_gather | solution.py:70
  62.3 161.7 %all-gather.19.cloned.1.call-start = ((), (), s32[]{:S(2)}) async-start(), calls=%async_computation.6 | async-start | bytes 1310720 | tf_op jit(solution)/shard_map/all_gather | solution.py:73
  62.9 226.1 %all-gather.9.cloned.1.call-start = ((), (), s32[]{:S(2)}) async-start(), calls=%async_computation.1 | async-start | bytes 3932160 | tf_op jit(solution)/shard_map/all_gather | solution.py:86
  63.4 247.5 %all-gather.21.cloned.1.call-start = ((), (), s32[]{:S(2)}) async-start(), calls=%async_computation.7 | async-start | bytes 2457600 | tf_op jit(solution)/shard_map/all_gather | solution.py:84
  88.4 117.5 %copy-start.3 = (bf16[4,32,384]{2,1,0:T(8,128)(2,1)S(1)}, bf16[4,32,384]{2,1,0:T(8,128)(2,1)}, u32[]{:S(2)}) copy-start(bf16[4,32,384]{2,1,0:T(8,128)(2,1)} %param.21) | copy-start | bytes 294916
  152.0 72.0 %copy-start.4 = (bf16[4,32,384]{2,1,0:T(8,128)(2,1)S(1)}, bf16[4,32,384]{2,1,0:T(8,128)(2,1)}, u32[]{:S(2)}) copy-start(bf16[4,32,384]{2,1,0:T(8,128)(2,1)} %param.23) | copy-start | bytes 294916
  216.1 18.9 %copy-start.1 = (bf16[4,384,32]{1,2,0:T(8,128)(2,1)S(1)}, bf16[4,384,32]{1,2,0:T(8,128)(2,1)}, u32[]{:S(2)}) copy-start(bf16[4,384,32]{1,2,0:T(8,128)(2,1)} %param.24) | copy-start | bytes 294916
  319.8 6.1 %copy-start.2 = (f32[64,8]{0,1:T(8,128)S(1)}, f32[64,8]{0,1:T(8,128)}, u32[]{:S(2)}) copy-start(f32[64,8]{0,1:T(8,128)} %param.15) | copy-start | bytes 6148
  321.1 36.3 %all-to-all-start = ((bf16[4,4,40,1024]{3,2,1,0:T(8,128)(2,1)}), bf16[4,4,40,1024]{3,2,1,0:T(8,128)(2,1)S(1)}, u32[]{:S(2)}, u32[]{:S(2)}) async-start(bf16[4,4,40,1024]{3,2,1,0:T(8,128)(2,1)} %copy.47), calls=%async_computation | async-start | bytes 2621440 | tf_op jit(solution)/shard_map/all_to_all | solution.py:92
Sparse Core Ops, SparseCore 0:
  8.9 74.5 all-gather.10
  85.0 62.0 all-gather.16
  148.6 15.3 all-gather.12
  165.4 40.3 all-gather.14
  207.3 16.6 all-gather.18
  225.4 63.4 all-gather.8
  290.5 20.4 all-gather.20
where the time goes:
time: 368 us
  waiting for transfers between devices  239 us (65%)
  blocking collectives  44.8 us (12%)
  matrix products  30.1 us (8%)
  other arithmetic  20.3 us (6%)
  local copies, waits for them, and re-layouts  15.1 us (4%)
  between operations  13.7 us (4%)
  starting transfers between devices  4.83 us (1%)
    all_gather x1, waiting for transfers between devices, shards(): base_rows_up = lax.all_gather(base_up, 'wide', axis=0, tiled=True)  58.7 us
    all_gather x1, waiting for transfers between devices, shards(): lax.all_gather(base_down, 'wide', axis=0, tiled=True)  47.3 us
    all_gather x1, waiting for transfers between devices, shards(): slot_rows = lax.all_gather(local_rows, 'narrow', axis=3, tiled=True)  41.9 us
    all_to_all x1, waiting for transfers between devices, shards(): lax.all_to_all(expert_out, 'wide', split_axis=0, concat_axis=0, tiled=True)  31.4 us
    all_gather x1, blocking collectives, shards(): every_row = lax.all_gather(tokens, 'wide', axis=0, tiled=True)  23.1 us
    all_gather x1, waiting for transfers between devices, shards(): base_rows_gate = lax.all_gather(base_gate, 'wide', axis=0, tiled=True)  20 us
    all_gather x1, waiting for transfers between devices, shards(): hidden_all = lax.all_gather(hidden, 'narrow', axis=3, tiled=True)  16.7 us
    convert_element_type x3, other arithmetic, rebuild(): return (base_rows.astype(jnp.float32)[None] + product).astype(jnp.bfloat16)  15.2 us
  transfers between devices with their start and end apart: 8, of which 8 were waited for; matrix products, arithmetic and copies ran while one was open for 14% of the time, Pallas kernels for 0%

commit v1 on v0

v1 whole, which is shorter than its diff:
```python
import jax
import jax.numpy as jnp
from jax import lax
from jax.sharding import PartitionSpec as P


def dot32(a, b):
    return jnp.dot(a, b, preferred_element_type=jnp.float32)


def shards(
    tokens,
    routes,
    gate_weights,
    delta_of,
    base_gate,
    base_up,
    base_down,
    gate_left,
    gate_right,
    up_left,
    up_right,
    down_left,
    down_right,
):
    exp_here, _, rank = gate_left.shape
    experts = delta_of.shape[0]
    mine = lax.axis_index("wide")
    bf16 = jnp.bfloat16

    expert_ids = lax.broadcasted_iota(jnp.int32, (1, 1, experts), 2)
    named = routes[:, :, None] == expert_ids
    delta_ids = jnp.sum(jnp.where(named, delta_of[None, None, :], 0), axis=2)
    weight_of = jnp.sum(
        jnp.where(delta_ids[:, :, None] == expert_ids, gate_weights[:, :, None], 0.0), axis=1
    )
    weights = lax.all_gather(weight_of, "wide", axis=0, tiled=True)
    weights = lax.dynamic_slice_in_dim(weights, mine * exp_here, exp_here, axis=1)

    rows = lax.all_gather(tokens, "wide", axis=0, tiled=True)
    full = lax.all_gather(rows, "narrow", axis=1, tiled=True)
    depth = base_gate.shape[0]
    part = lax.dynamic_slice_in_dim(full, mine * depth, depth, axis=1)

    base_both = jnp.concatenate([base_gate, base_up], axis=1)
    both = lax.psum(dot32(part, base_both), "wide")
    columns = base_gate.shape[1]

    lefts = jnp.concatenate([gate_left, up_left], axis=0)
    low = lax.psum(jnp.einsum("td,edr->ter", rows, lefts, preferred_element_type=jnp.float32), "narrow")
    low = low.astype(bf16)

    mixed = 0.0
    thin = []
    for e in range(exp_here):
        gate = both[:, :columns] + dot32(low[:, e], gate_right[e])
        up = both[:, columns:] + dot32(low[:, exp_here + e], up_right[e])
        hidden = jax.nn.silu(gate) * up * weights[:, e : e + 1]
        mixed = mixed + hidden
        thin.append(dot32(hidden.astype(bf16), down_left[e]))
    mixed = lax.psum(mixed, "wide").astype(bf16)
    mixed_full = lax.all_gather(mixed, "narrow", axis=1, tiled=True)
    depth = base_down.shape[0]
    mixed_part = lax.dynamic_slice_in_dim(mixed_full, mine * depth, depth, axis=1)
    thin = lax.psum(jnp.concatenate(thin, axis=1), "narrow").astype(bf16)
    out = dot32(mixed_part, base_down) + dot32(thin, down_right.reshape(exp_here * rank, -1))
    out = lax.psum_scatter(out, "wide", scatter_dimension=0, tiled=True)
    return out.astype(bf16)


def solution(mesh):
    return jax.shard_map(
        shards,
        mesh=mesh,
        in_specs=(
            P(("groups", "wide"), "narrow"),
            P(("groups", "wide"), None),
            P(("groups", "wide"), None),
            P(),
            P("wide", "narrow"),
            P("wide", "narrow"),
            P("wide", "narrow"),
            P("wide", "narrow", None),
            P("wide", None, "narrow"),
            P("wide", "narrow", None),
            P("wide", None, "narrow"),
            P("wide", "narrow", None),
            P("wide", None, "narrow"),
        ),
        out_specs=P(("groups", "wide"), "narrow"),
        check_vma=False,
    )
```

time: 368 us -> 181 us (0.49)
  waiting for transfers between devices: 239 us -> 64.2 us
  blocking collectives: 44.8 us -> 91.1 us
  matrix products: 30.1 us -> 9.89 us
  other arithmetic: 20.3 us -> 1.75 us
  local copies, waits for them, and re-layouts: 15.1 us -> 0.39 us
  starting transfers between devices: 4.83 us -> 0.09 us
    all_gather x7 -> x1, waiting for transfers between devices: 204 us -> 22.3 us  [shards(): full = lax.all_gather(rows, 'narrow', axis=1, tiled=True)]
    psum x0 -> x3, blocking collectives: none -> 50.7 us  [the longest x1 25.1 us: shards(): mixed = lax.psum(mixed, 'wide').astype(bf16)]
    all_to_all x1 -> x0, waiting for transfers between devices: 31.4 us -> none  [shards(): lax.all_to_all(expert_out, 'wide', split_axis=0, concat_axis=0, tiled=True)]
    reduce_scatter x0 -> x1, waiting for transfers between devices: none -> 25.9 us  [shards(): out = lax.psum_scatter(out, 'wide', scatter_dimension=0, tiled=True)]
    dot_general x4 -> x16, matrix products: 30.1 us -> 9.89 us  [the longest x15 9.54 us: dot32(): return jnp.dot(a, b, preferred_element_type=jnp.float32)]
    psum x0 -> x1, waiting for transfers between devices: none -> 15.9 us  [shards(): both = lax.psum(dot32(part, base_both), 'wide')]
    convert_element_type x4 -> x1, other arithmetic: 15.9 us -> 1.62 us  [shards(): return out.astype(bf16)]
    scatter x1 -> x0, local copies, waits for them, and re-layouts: 8.04 us -> none  [shards(): picked_rows = jnp.full((slot_total,), every_row.shape[0], jnp.int32).at[t...]
  transfers between devices with their start and end apart: 8 -> 3, of which waited for: 8 -> 3; matrix products, arithmetic and copies ran while one was open for 14% -> 0% of each run, Pallas kernels for 0% -> 0%
where the time goes in v1:
time: 181 us
  blocking collectives  91.1 us (50%)
  waiting for transfers between devices  64.2 us (35%)
  between operations  13.4 us (7%)
  matrix products  9.89 us (5%)
    reduce_scatter x1, waiting for transfers between devices, shards(): out = lax.psum_scatter(out, 'wide', scatter_dimension=0, tiled=True)  25.9 us
    psum x1, blocking collectives, shards(): mixed = lax.psum(mixed, 'wide').astype(bf16)  25.1 us
    all_gather x1, waiting for transfers between devices, shards(): full = lax.all_gather(rows, 'narrow', axis=1, tiled=True)  22.3 us
    all_gather x1, blocking collectives, shards(): rows = lax.all_gather(tokens, 'wide', axis=0, tiled=True)  19.5 us
    psum x1, waiting for transfers between devices, shards(): both = lax.psum(dot32(part, base_both), 'wide')  15.9 us
    psum x1, blocking collectives, shards(): lax.psum(jnp.einsum('td,edr->ter', rows, lefts, preferred_element_type=jn...  13.8 us
    all_gather x1, blocking collectives, shards(): weights = lax.all_gather(weight_of, 'wide', axis=0, tiled=True)  13.5 us
    psum x1, blocking collectives, shards(): thin = lax.psum(jnp.concatenate(thin, axis=1), 'narrow').astype(bf16)  11.8 us
  transfers between devices with their start and end apart: 3, of which 3 were waited for; matrix products, arithmetic and copies ran while one was open for 0% of the time, Pallas kernels for 0%

profile of v1, /device:TPU:0, one launch (start us, length us, event | category | flops | bytes accessed | tf_op | source)
XLA Modules:
  0.0 180.8 jit_solution(11253720552039283029)
XLA Ops:
  6.5 0.0 copy-start
  6.5 0.0 all-gather.3.cloned.1.call-start
  6.5 19.5 %all_gather.12 = bf16[256,1024]{1,0:T(8,128)(2,1)} all-gather(bf16[64,1024]{1,0:T(8,128)(2,1)} %param.13), channel_id=1, replica_groups=mesh['groups'=2,'wide'=4,'narrow'=4] {'wide'}, dimensions={0}, use_global_device_ids=true | all-gather | bytes 655360 | tf_op jit(solution)/shard_map/all_gather | solution.py:40
  26.0 0.0 all-gather.3.cloned.1.call-update
  26.0 0.0 all-reduce.5.cloned.1.call-start
  26.1 0.0 copy-start.2
  26.1 0.0 copy-start.10
  26.1 0.0 copy-start.11
  26.1 22.3 %all-gather.3.cloned.1.call-done = bf16[256,4096]{1,0:T(8,128)(2,1)} async-done(((bf16[256,1024]{1,0:T(8,128)(2,1)}), bf16[256,4096]{1,0:T(8,128)(2,1)}) %all-gather.3.cloned.1.call-update) | async-done | bytes 2097168 | tf_op jit(solution)/shard_map/all_gather | solution.py:41
  48.5 3.0 %fusion = f32[256,768]{1,0:T(8,128)} fusion(bf16[1024,384]{1,0:T(8,128)(2,1)} %param.18, bf16[1024,384]{1,0:T(8,128)(2,1)} %param.17, bf16[256,4096]{1,0:T(8,128)(2,1)} %all-gather.3.cloned.1.call-done, s32[]{:T(128)S(6)} %select_n.17), kind=kOutput, calls=%fused_computation | convolution fusion | flops 405798912 | bytes 2883588 | tf_op jit(solution)/shard_map/dot_general | solution.py:8
  51.5 0.0 copy-start.7
  51.5 0.0 copy-start.9
  51.5 0.0 copy-start.8
  51.5 0.0 copy-start.4
  51.5 0.0 copy-start.6
  51.5 0.0 all-reduce.5.cloned.1.call-update
  51.5 0.0 reduce-scatter.2.cloned.1.call-start
  51.6 0.0 copy-done.2
  51.6 0.0 copy-done.10
  51.6 0.0 copy-done.11
  51.6 0.3 convolution_bitcast_fusion
  52.0 0.2 copy-done.7
  52.2 0.0 copy-done.9
  52.2 0.0 copy-start.5
  52.2 0.1 select_reduce_fusion.1
  52.3 0.0 copy-done.8
  52.3 13.5 %all-gather = f32[4,64,16]{1,2,0:T(8,128)S(1)} all-gather(f32[1,64,16]{1,2,0:T(8,128)S(1)} %bitcast.82), channel_id=1, replica_groups=mesh['groups'=2,'wide'=4,'narrow'=4] {'wide'}, dimensions={0}, use_global_device_ids=true | all-gather | bytes 20480 | tf_op jit(solution)/shard_map/all_gather | solution.py:37
  65.8 0.1 reshape.9
  65.9 13.8 %all-reduce.6 = bf16[256,8,32]{0,2,1:T(8,128)(2,1)S(1)} all-reduce(f32[256,8,32]{0,2,1:T(8,128)S(1)} %convolution_bitcast_fusion), channel_id=1, replica_groups=mesh['groups'=2,'wide'=4,'narrow'=4] {'narrow'}, use_global_device_ids=true, to_apply=%region_1.2 | all-reduce | flops 65536 | bytes 393216 | tf_op jit(solution)/shard_map/psum | solution.py:50
  79.8 15.9 %all-reduce.5.cloned.1.call-done = f32[256,768]{1,0:T(8,128)} async-done(((f32[256,768]{1,0:T(8,128)}), f32[256,768]{1,0:T(8,128)}) %all-reduce.5.cloned.1.call-update) | async-done | bytes 786448 | tf_op jit(solution)/shard_map/psum | solution.py:46
  95.7 0.0 copy-done.4
  95.7 0.0 copy-start.1
  95.7 1.3 convolution_add_fusion.4
  97.0 0.0 copy-done.6
  97.0 1.3 fusion.10
  98.2 0.0 copy-done.5
  98.3 0.2 fusion.19
  98.4 0.0 copy-done.1
  98.4 0.2 convolution_add_fusion.6
  98.7 0.3 fusion.9
  99.0 0.2 fusion.21
  99.1 0.3 convolution_add_fusion.8
  99.4 0.3 fusion.8
  99.7 0.2 fusion.23
  99.9 0.3 convolution_add_fusion.2
  100.1 0.0 copy-start.3
  100.1 0.3 add_add_fusion
  100.5 0.2 fusion.17
  100.7 11.8 %all-reduce.7 = bf16[256,128]{0,1:T(8,128)(2,1)S(1)} all-reduce(f32[256,128]{0,1:T(8,128)S(1)} %pad_maximum_fusion), channel_id=1, replica_groups=mesh['groups'=2,'wide'=4,'narrow'=4] {'narrow'}, use_global_device_ids=true, to_apply=%region_5.6 | all-reduce | flops 32768 | bytes 196608 | tf_op jit(solution)/shard_map/psum | solution.py:65
  112.5 25.1 %all-reduce.8 = bf16[256,384]{1,0:T(8,128)(2,1)S(1)} all-reduce(f32[256,384]{1,0:T(8,128)S(1)} %get-tuple-element.9), channel_id=1, replica_groups=mesh['groups'=2,'wide'=4,'narrow'=4] {'wide'}, use_global_device_ids=true, to_apply=%region_4.5 | all-reduce | flops 98304 | bytes 589824 | tf_op jit(solution)/shard_map/psum | solution.py:61
  137.6 7.4 %all_gather.15 = bf16[256,1536]{1,0:T(8,128)(2,1)S(1)} all-gather(bf16[256,384]{1,0:T(8,128)(2,1)S(1)} %all-reduce.8), channel_id=1, replica_groups=mesh['groups'=2,'wide'=4,'narrow'=4] {'narrow'}, dimensions={1}, use_global_device_ids=true | all-gather | bytes 983040 | tf_op jit(solution)/shard_map/all_gather | solution.py:62
  145.0 0.0 copy-done.3
  145.0 0.3 fusion.56
  145.3 0.0 copy-done
  145.3 1.4 convolution_add_fusion
  146.7 0.0 reduce-scatter.2.cloned.1.call-update
  146.8 25.9 %reduce-scatter.2.cloned.1.call-done = f32[64,1024]{1,0:T(8,128)} async-done(((f32[256,1024]{1,0:T(8,128)}), f32[64,1024]{1,0:T(8,128)}) %reduce-scatter.2.cloned.1.call-update) | async-done | bytes 262160 | tf_op jit(solution)/shard_map/reduce_scatter | solution.py:67
  172.7 1.6 convert_element_type.31
  (4 shorter events, 0.1 us)
Async XLA Ops:
  6.5 138.8 %copy-start = (bf16[384,1024]{1,0:T(8,128)(2,1)S(1)}, bf16[384,1024]{1,0:T(8,128)(2,1)}, u32[]{:S(2)}) copy-start(bf16[384,1024]{1,0:T(8,128)(2,1)} %param.19) | copy-start | bytes 2359300
  6.5 41.9 %all-gather.3.cloned.1.call-start = ((), (), s32[]{:S(2)}) async-start(), calls=%async_computation.1 | async-start | bytes 2621440 | tf_op jit(solution)/shard_map/all_gather | solution.py:41
  26.0 69.6 %all-reduce.5.cloned.1.call-start = ((), (), s32[]{:S(2)}) async-start(), calls=%async_computation.2 | async-start | bytes 1572864 | tf_op jit(solution)/shard_map/psum | solution.py:46
  26.1 25.5 %copy-start.2 = (bf16[256,1024]{1,0:T(8,128)(2,1)S(1)}, bf16[256,1024]{1,0:T(8,128)(2,1)}, u32[]{:S(2)}) copy-start(bf16[256,1024]{1,0:T(8,128)(2,1)} %all_gather.12) | copy-start | bytes 1572868
  26.1 25.5 %copy-start.10 = (bf16[4,1024,32]{1,2,0:T(8,128)(2,1)S(1)}, bf16[4,1024,32]{1,2,0:T(8,128)(2,1)}, u32[]{:S(2)}) copy-start(bf16[4,1024,32]{1,2,0:T(8,128)(2,1)} %param.22) | copy-start | bytes 786436
  26.1 25.5 %copy-start.11 = (bf16[4,1024,32]{1,2,0:T(8,128)(2,1)S(1)}, bf16[4,1024,32]{1,2,0:T(8,128)(2,1)}, u32[]{:S(2)}) copy-start(bf16[4,1024,32]{1,2,0:T(8,128)(2,1)} %param.20) | copy-start | bytes 786436
  51.5 0.7 copy-start.7
  51.5 0.7 copy-start.9
  51.5 0.8 copy-start.8
  51.5 44.2 %copy-start.4 = (bf16[4,32,384]{2,1,0:T(8,128)(2,1)S(1)}, bf16[4,32,384]{2,1,0:T(8,128)(2,1)}, u32[]{:S(2)}) copy-start(bf16[4,32,384]{2,1,0:T(8,128)(2,1)} %param.21) | copy-start | bytes 294916
  51.5 45.5 %copy-start.6 = (bf16[4,32,384]{2,1,0:T(8,128)(2,1)S(1)}, bf16[4,32,384]{2,1,0:T(8,128)(2,1)}, u32[]{:S(2)}) copy-start(bf16[4,32,384]{2,1,0:T(8,128)(2,1)} %param.23) | copy-start | bytes 294916
  51.5 121.1 %reduce-scatter.2.cloned.1.call-start = ((), (), s32[]{:S(2)}) async-start(), calls=%async_computation.3 | async-start | bytes 1310720 | tf_op jit(solution)/shard_map/reduce_scatter | solution.py:67
  52.2 46.1 %copy-start.5 = (bf16[4,384,32]{1,2,0:T(8,128)(2,1)S(1)}, bf16[4,384,32]{1,2,0:T(8,128)(2,1)}, u32[]{:S(2)}) copy-start(bf16[4,384,32]{1,2,0:T(8,128)(2,1)} %param.24) | copy-start | bytes 294916
  95.7 2.8 %copy-start.1 = (f32[256,768]{1,0:T(8,128)S(1)}, f32[256,768]{1,0:T(8,128)}, u32[]{:S(2)}) copy-start(f32[256,768]{1,0:T(8,128)} %all-reduce.5.cloned.1.call-done) | copy-start | bytes 2359300
  100.1 44.9 %copy-start.3 = (bf16[4,32,1024]{2,1,0:T(8,128)(2,1)S(1)}, bf16[4,32,1024]{2,1,0:T(8,128)(2,1)}, u32[]{:S(2)}) copy-start(bf16[4,32,1024]{2,1,0:T(8,128)(2,1)} %param.25) | copy-start | bytes 786436
Sparse Core Ops, SparseCore 0:
  26.2 22.2 all-gather.2
  51.6 43.9 all-reduce.4
  146.9 25.7 reduce-scatter.1

commit v2 on v1

--- a/solution.py
+++ b/solution.py
@@ -1,11 +1,295 @@
 import jax
 import jax.numpy as jnp
 from jax import lax
+from jax.experimental import pallas as pl
+from jax.experimental.pallas import tpu as pltpu
 from jax.sharding import PartitionSpec as P
 
 
 def dot32(a, b):
     return jnp.dot(a, b, preferred_element_type=jnp.float32)
+
+
+PLANE = 4
+
+
+def kernel(
+    tok, wt, bg, bu, bd, gl, gr, ul, ur, dl, dr, out,
+    xcol, xw, wts, gsend, grecv, gown, gred, gall, apart, asend, arecv, afin,
+    hacc, hsend, hrecv, hpl, bpart, bsend, brecv, bfin, osend, orecv, oown,
+    tok_s, tok_r, wt_s, wt_r, bs_s, bs_r, g_s, g_r, ga_s, ga_r, a_s, a_r,
+    h_s, h_r, hb_s, hb_r, b_s, b_r, o_s, o_r,
+):
+    bf16, f32 = jnp.bfloat16, jnp.float32
+    count = PLANE
+    w, n = lax.axis_index("wide"), lax.axis_index("narrow")
+    exp_here, rank = gl.shape[0], gl.shape[2]
+    cols = bg.shape[1]
+    span = exp_here * rank
+    pair = n + 1 - 2 * lax.rem(n, 2)
+    across = lax.rem(n + 2, count)
+    root = n == w
+    relay = n == lax.rem(w + 2, count)
+
+    def up_of(d):
+        return lax.rem(w + d, count)
+
+    def copy(src, dst, ss, rs, axis, peer):
+        return pltpu.make_async_remote_copy(
+            src_ref=src, dst_ref=dst, send_sem=ss, recv_sem=rs,
+            device_id={axis: peer}, device_id_type=pl.DeviceIdType.MESH,
+        )
+
+    barrier = pltpu.get_barrier_semaphore()
+    for d in range(1, count):
+        pl.semaphore_signal(barrier, inc=1, device_id={"wide": up_of(d)}, device_id_type=pl.DeviceIdType.MESH)
+    for peer in (pair, across):
+        pl.semaphore_signal(barrier, inc=1, device_id={"narrow": peer}, device_id_type=pl.DeviceIdType.MESH)
+    pl.semaphore_wait(barrier, count + 1)
+
+    def tok_copy(d):
+        return copy(tok, xcol.at[w], tok_s.at[d], tok_r.at[d], "wide", up_of(d))
+
+    def wt_copy(d):
+        return copy(wt, wts.at[w], wt_s.at[d], wt_r.at[d], "wide", up_of(d))
+
+    def pair_copy(d, src):
+        return copy(src, xw.at[up_of(count - d)], bs_s.at[d, 0], bs_r.at[d], "narrow", pair)
+
+    def across_copy(d, src):
+        return copy(src, xw.at[up_of(count - d)], bs_s.at[d, 1], bs_r.at[d], "narrow", across)
+
+    for d in range(1, count):
+        tok_copy(d).start()
+
+    def low(rows, b):
+        for e in range(exp_here):
+            apart[b, :, e * rank : (e + 1) * rank] = dot32(rows, gl[e])
+            apart[b, :, span + e * rank : span + (e + 1) * rank] = dot32(rows, ul[e])
+
+    for d in range(count):
+        b = up_of(count - d)
+        if d > 0:
+            tok_copy(d).wait_recv()
+        mine = tok if d == 0 else xcol.at[b]
+
+        @pl.when(root)
+        def _():
+            across_copy(d, mine).start()
+            pair_copy(d, mine).start()
+            xw[b] = mine[...]
+
+        low(mine[...], b)
+
+        @pl.when(jnp.logical_not(root))
+        def _():
+            pair_copy(d, xw.at[b]).wait_recv()
+
+        @pl.when(relay)
+        def _():
+            pair_copy(d, xw.at[b]).start()
+
+        rows = xw[b]
+        gate, up = dot32(rows, bg[...]), dot32(rows, bu[...])
+        if d == 0:
+            gown[:, :cols] = gate
+            gown[:, cols:] = up
+            for k in range(1, count):
+                wt_copy(k).start()
+        else:
+            gsend[b, :, :cols] = gate.astype(bf16)
+            gsend[b, :, cols:] = up.astype(bf16)
+            copy(gsend.at[b], grecv.at[w], g_s.at[d], g_r.at[d], "wide", b).start()
+
+    def a_copy(k):
+        return copy(asend.at[k], arecv.at[k], a_s.at[k], a_r.at[k], "narrow", (pair, across)[k])
+
+    asend[0] = apart[...].astype(bf16)
+    a_copy(0).start()
+    a_copy(0).wait_recv()
+    apart[...] = apart[...] + arecv[0].astype(f32)
+    asend[1] = apart[...].astype(bf16)
+    a_copy(1).start()
+
+    def ga_copy(d):
+        return copy(gred, gall.at[w], ga_s.at[d], ga_r.at[d], "wide", up_of(d))
+
+    total = gown[...]
+    for d in range(1, count):
+        s = up_of(d)
+        copy(gsend.at[s], grecv.at[s], g_s.at[d], g_r.at[d], "wide", s).wait_recv()
+        total = total + grecv[s].astype(f32)
+    gown[...] = total
+    gred[...] = total.astype(bf16)
+    for d in range(1, count):
+        ga_copy(d).start()
+
+    a_copy(1).wait_recv()
+    afin[...] = (apart[...] + arecv[1].astype(f32)).astype(bf16)
+
+    for d in range(count):
+        b = up_of(count - d)
+        if d > 0:
+            ga_copy(d).wait_recv()
+            wt_copy(d).wait_recv()
+            gates, ups = gall[b, :, :cols].astype(f32), gall[b, :, cols:].astype(f32)
+            scales = wts[b]
+        else:
+            gates, ups = gown[:, :cols], gown[:, cols:]
+            scales = wt[...]
+        ids = lax.broadcasted_iota(jnp.int32, scales.shape, 1)
+        thin_rows = afin[b]
+        acc = None
+        for e in range(exp_here):
+            scale = jnp.sum(jnp.where(ids == w * exp_here + e, scales, 0.0), axis=1, keepdims=True)
+            gate = gates + dot32(thin_rows[:, e * rank : (e + 1) * rank], gr[e])
+            up = ups + dot32(thin_rows[:, span + e * rank : span + (e + 1) * rank], ur[e])
+            hidden = gate / (1.0 + jnp.exp(-gate)) * up * scale
+            acc = hidden if acc is None else acc + hidden
+            bpart[b, :, e * rank : (e + 1) * rank] = dot32(hidden.astype(bf16), dl[e])
+        hacc[b] = acc
+        hsend[b] = acc.astype(bf16)
+
+    def h_copy(slot, target):
+        return copy(hsend, hrecv.at[slot], h_s, h_r.at[slot], "wide", target)
+
+    @pl.when(jnp.logical_not(root))
+    def _():
+        h_copy(w, n).start()
+
+    def b_copy(k):
+        return copy(bsend.at[k], brecv.at[k], b_s.at[k], b_r.at[k], "narrow", (pair, across)[k])
+
+    bsend[0] = bpart[...].astype(bf16)
+    b_copy(0).start()
+    b_copy(0).wait_recv()
+    bpart[...] = bpart[...] + brecv[0].astype(f32)
+    bsend[1] = bpart[...].astype(bf16)
+    b_copy(1).start()
+    b_copy(1).wait_recv()
+    bfin[...] = (bpart[...] + brecv[1].astype(f32)).astype(bf16)
+
+    def hpair():
+        return copy(hpl, hpl, hb_s.at[0], hb_r, "narrow", pair)
+
+    def hacross():
+        return copy(hpl, hpl, hb_s.at[1], hb_r, "narrow", across)
+
+    @pl.when(root)
+    def _():
+        whole = hacc[...]
+        for d in range(1, count):
+            s = up_of(d)
+            h_copy(s, s).wait_recv()
+            whole = whole + hrecv[s].astype(f32)
+        hpl[...] = whole.astype(bf16)
+        hacross().start()
+        hpair().start()
+
+    @pl.when(jnp.logical_not(root))
+    def _():
+        hpair().wait_recv()
+
+    @pl.when(relay)
+    def _():
+        hpair().start()
+
+    for d in (2, 1, 3, 0):
+        b = up_of(count - d)
+        part = dot32(hpl[b], bd[...]) + dot32(bfin[b], dr[...])
+        if d == 0:
+            oown[...] = part
+        else:
+            osend[b] = part.astype(bf16)
+            copy(osend.at[b], orecv.at[w], o_s.at[d], o_r.at[d], "wide", b).start()
+    total = oown[...]
+    for d in (1, 3, 2):
+        s = up_of(d)
+        copy(osend.at[s], orecv.at[s], o_s.at[d], o_r.at[d], "wide", s).wait_recv()
+        total = total + orecv[s].astype(f32)
+    out[...] = total.astype(bf16)
+
+    for d in range(1, count):
+        b = up_of(count - d)
+        tok_copy(d).wait_send()
+        wt_copy(d).wait_send()
+        ga_copy(d).wait_send()
+        copy(gsend.at[b], grecv.at[w], g_s.at[d], g_r.at[d], "wide", b).wait_send()
+        copy(osend.at[b], orecv.at[w], o_s.at[d], o_r.at[d], "wide", b).wait_send()
+    for k in range(2):
+        a_copy(k).wait_send()
+        b_copy(k).wait_send()
+
+    @pl.when(root)
+    def _():
+        for d in range(count):
+            src = tok if d == 0 else xcol.at[up_of(count - d)]
+            across_copy(d, src).wait_send()
+            pair_copy(d, src).wait_send()
+        hacross().wait_send()
+        hpair().wait_send()
+
+    @pl.when(relay)
+    def _():
+        for d in range(count):
+            pair_copy(d, xw.at[up_of(count - d)]).wait_send()
+        hpair().wait_send()
+
+    @pl.when(jnp.logical_not(root))
+    def _():
+        h_copy(w, n).wait_send()
+
+
+def fused(tokens, weight_of, bg, bu, bd, gl, gr, ul, ur, dl, dr):
+    bf16, f32 = jnp.bfloat16, jnp.float32
+    count = PLANE
+    rows, feats = tokens.shape
+    cols = bg.shape[1]
+    exp_here, rank = gl.shape[0], gl.shape[2]
+    span = exp_here * rank
+    lanes = -(-weight_of.shape[1] // 128) * 128
+    wt = jnp.pad(weight_of, ((0, 0), (0, lanes - weight_of.shape[1])))
+    sem = pltpu.SemaphoreType.DMA
+    vm = pltpu.VMEM
+    out_feats = bd.shape[1]
+    return pl.pallas_call(
+        kernel,
+        out_shape=jax.ShapeDtypeStruct((rows, out_feats), bf16),
+        in_specs=[pl.BlockSpec(memory_space=pltpu.VMEM)] * 11,
+        out_specs=pl.BlockSpec(memory_space=pltpu.VMEM),
+        scratch_shapes=[
+            vm((count, rows, feats), bf16),
+            vm((count, rows, feats), bf16),
+            vm((count, rows, lanes), f32),
+            vm((count, rows, 2 * cols), bf16),
+            vm((count, rows, 2 * cols), bf16),
+            vm((rows, 2 * cols), f32),
+            vm((rows, 2 * cols), bf16),
+            vm((count, rows, 2 * cols), bf16),
+            vm((count, rows, 2 * span), f32),
+            vm((2, count, rows, 2 * span), bf16),
+            vm((2, count, rows, 2 * span), bf16),
+            vm((count, rows, 2 * span), bf16),
+            vm((count, rows, cols), f32),
+            vm((count, rows, cols), bf16),
+            vm((count, count, rows, cols), bf16),
+            vm((count, rows, cols), bf16),
+            vm((count, rows, span), f32),
+            vm((2, count, rows, span), bf16),
+            vm((2, count, rows, span), bf16),
+            vm((count, rows, span), bf16),
+            vm((count, rows, out_feats), bf16),
+            vm((count, rows, out_feats), bf16),
+            vm((rows, out_feats), f32),
+            sem((count,)), sem((count,)), sem((count,)), sem((count,)),
+            sem((count, 2)), sem((count,)),
+            sem((count,)), sem((count,)), sem((count,)), sem((count,)),
+            sem((2,)), sem((2,)),
+            sem, sem((count,)), sem((2,)), sem,
+            sem((2,)), sem((2,)), sem((count,)), sem((count,)),
+        ],
+        compiler_params=pltpu.CompilerParams(collective_id=0, has_side_effects=True, vmem_limit_bytes=60 * 1024 * 1024),
+    )(tokens, wt, bg, bu, bd, gl, gr, ul, ur, dl, dr.reshape(span, out_feats))
 
 
 def shards(
@@ -34,6 +318,8 @@
     weight_of = jnp.sum(
         jnp.where(delta_ids[:, :, None] == expert_ids, gate_weights[:, :, None], 0.0), axis=1
     )
+    if lax.axis_size("narrow") == PLANE and lax.axis_size("wide") == PLANE:
+        return fused(tokens, weight_of, base_gate, base_up, base_down, gate_left, gate_right, up_left, up_right, down_left, down_right)
     weights = lax.all_gather(weight_of, "wide", axis=0, tiled=True)
     weights = lax.dynamic_slice_in_dim(weights, mine * exp_here, exp_here, axis=1)
 

time: 181 us -> 75.8 us (0.42)
  blocking collectives: 91.1 us -> 0 us
  Pallas kernels: 0 us -> 67.5 us
  waiting for transfers between devices: 64.2 us -> 0 us
  between operations: 13.4 us -> 0.02 us
  matrix products: 9.89 us -> 0 us
  local copies, waits for them, and re-layouts: 0.39 us -> 5.95 us
    pallas_call x0 -> x1, Pallas kernels: none -> 67.5 us  [fused(): pl.pallas_call(kernel, out_shape=jax.ShapeDtypeStruct((rows, out_feats),...]
    psum x3 -> x0, blocking collectives: 50.7 us -> none  [the longest x1 25.1 us: shards(): mixed = lax.psum(mixed, 'wide').astype(bf16)]
    all_gather x3 -> x0, blocking collectives: 40.4 us -> none  [the longest x1 19.5 us: shards(): rows = lax.all_gather(tokens, 'wide', axis=0, tiled=True)]
    reduce_scatter x1 -> x0, waiting for transfers between devices: 25.9 us -> none  [shards(): out = lax.psum_scatter(out, 'wide', scatter_dimension=0, tiled=True)]
    all_gather x1 -> x0, waiting for transfers between devices: 22.3 us -> none  [shards(): full = lax.all_gather(rows, 'narrow', axis=1, tiled=True)]
    psum x1 -> x0, waiting for transfers between devices: 15.9 us -> none  [shards(): both = lax.psum(dot32(part, base_both), 'wide')]
    dot_general x16 -> x0, matrix products: 9.89 us -> none  [the longest x15 9.54 us: dot32(): return jnp.dot(a, b, preferred_element_type=jnp.float32)]
    unnamed x25 -> x10, local copies, waits for them, and re-layouts: 0.36 us -> 5.24 us
  transfers between devices with their start and end apart: 3 -> 0, of which waited for: 3 -> 0; matrix products, arithmetic and copies ran while one was open for 0% -> 0% of each run, Pallas kernels for 0% -> 0%
where the time goes in v2:
time: 75.8 us; the launch traced here: 75 us
  Pallas kernels  67.5 us (89%)
  local copies, waits for them, and re-layouts  5.95 us (8%)
  other arithmetic  1.53 us (2%)
    pallas_call x1, Pallas kernels, fused(): pl.pallas_call(kernel, out_shape=jax.ShapeDtypeStruct((rows, out_feats),...  67.5 us
    unnamed x10, local copies, waits for them, and re-layouts  5.24 us

profile of v2, /device:TPU:0, one launch (start us, length us, event | category | flops | bytes accessed | tf_op | source)
XLA Modules:
  0.0 75.0 jit_solution(1565411537185464271)
XLA Ops:
  0.0 0.0 copy-start.2
  0.0 0.8 %select_reduce_fusion.1 = s32[64,8]{0,1:T(8,128)S(1)} fusion(s32[16]{0:T(128)} %param.16, s32[64,8]{0,1:T(8,128)} %param.14), kind=kLoop, calls=%fused_computation.2 | loop fusion | flops 24064 | bytes 4160 | tf_op jit(solution)/shard_map/reduce_sum | solution.py:317
  0.8 0.7 select_reduce_fusion
  1.5 0.1 copy.19
  1.6 0.6 pad.4.wt
  2.2 0.0 copy-done.2
  2.2 0.0 copy-start
  2.2 0.9 %copy.22.dl = bf16[4,384,32]{2,1,0:T(8,128)(2,1)} copy(bf16[4,384,32]{1,2,0:T(8,128)(2,1)S(1)} %copy-done.2) | data formatting | bytes 196608 | tf_op args[11]
  3.2 0.0 copy-done
  3.2 0.0 copy-start.1
  3.2 1.3 %copy.20.gl = bf16[4,1024,32]{2,1,0:T(8,128)(2,1)} copy(bf16[4,1024,32]{1,2,0:T(8,128)(2,1)S(1)} %copy-done) | data formatting | bytes 524288 | tf_op args[7]
  4.5 0.0 copy-done.1
  4.5 1.4 %copy.21.ul = bf16[4,1024,32]{2,1,0:T(8,128)(2,1)} copy(bf16[4,1024,32]{1,2,0:T(8,128)(2,1)S(1)} %copy-done.1) | data formatting | bytes 524288 | tf_op args[9]
  5.9 67.5 %shard_map.127 = bf16[64,1024]{1,0:T(8,128)(2,1)} custom-call(bf16[64,1024]{1,0:T(8,128)(2,1)} %tok.1, f32[64,128]{1,0:T(8,128)} %pad.4.wt, bf16[1024,384]{1,0:T(8,128)(2,1)} %bg.1, bf16[1024,384]{1,0:T(8,128)(2,1)} %bu.1, bf16[384,1024]{1,0:T(8,128)(2,1)} %bd.1, bf16[4,1024,32]{2,1,0:T(8,128)(2,1)} %copy.20.gl, bf16[4,32,384]{2,1,0:T(8,128)(2,1)} %gr.1, ...), custom_call_target="tpu_custom_call" | custom-call | tf_op jit(solution)/shard_map/pallas_call | solution.py:255
  73.4 1.6 %copy.24 = bf16[64,1024]{1,0:T(8,128)(2,1)} copy(bf16[64,1024]{1,0:T(8,128)(2,1)} %shard_map.127) | data formatting | bytes 262144
Async XLA Ops:
  0.0 2.2 %copy-start.2 = (bf16[4,384,32]{1,2,0:T(8,128)(2,1)S(1)}, bf16[4,384,32]{1,2,0:T(8,128)(2,1)}, u32[]{:S(2)}) copy-start(bf16[4,384,32]{1,2,0:T(8,128)(2,1)} %param.24) | copy-start | bytes 294916
  2.2 1.0 %copy-start = (bf16[4,1024,32]{1,2,0:T(8,128)(2,1)S(1)}, bf16[4,1024,32]{1,2,0:T(8,128)(2,1)}, u32[]{:S(2)}) copy-start(bf16[4,1024,32]{1,2,0:T(8,128)(2,1)} %param.20) | copy-start | bytes 786436
  3.2 1.3 %copy-start.1 = (bf16[4,1024,32]{1,2,0:T(8,128)(2,1)S(1)}, bf16[4,1024,32]{1,2,0:T(8,128)(2,1)}, u32[]{:S(2)}) copy-start(bf16[4,1024,32]{1,2,0:T(8,128)(2,1)} %param.22) | copy-start | bytes 786436

commit v3 on v2

--- a/solution.py
+++ b/solution.py
@@ -10,22 +10,36 @@
     return jnp.dot(a, b, preferred_element_type=jnp.float32)
 
 
+def dot32t(a, b):
+    return lax.dot_general(a, b, (((1,), (1,)), ((), ())), preferred_element_type=jnp.float32)
+
+
 PLANE = 4
 
 
 def kernel(
-    tok, wt, bg, bu, bd, gl, gr, ul, ur, dl, dr, out,
+    tok, routes, shares, delta, bg_hbm, bu_hbm, bd_hbm, gl_hbm, gr, ul_hbm, ur, dl, dr_hbm, out,
+    wt, bgu, lefts, bd, dr,
     xcol, xw, wts, gsend, grecv, gown, gred, gall, apart, asend, arecv, afin,
     hacc, hsend, hrecv, hpl, bpart, bsend, brecv, bfin, osend, orecv, oown,
     tok_s, tok_r, wt_s, wt_r, bs_s, bs_r, g_s, g_r, ga_s, ga_r, a_s, a_r,
-    h_s, h_r, hb_s, hb_r, b_s, b_r, o_s, o_r,
+    h_s, h_r, hb_s, hb_r, b_s, b_r, o_s, o_r, in_s,
 ):
     bf16, f32 = jnp.bfloat16, jnp.float32
     count = PLANE
     w, n = lax.axis_index("wide"), lax.axis_index("narrow")
-    exp_here, rank = gl.shape[0], gl.shape[2]
-    cols = bg.shape[1]
+    exp_here, rank, cols = gr.shape
     span = exp_here * rank
+    loads = [
+        pltpu.make_async_copy(gl_hbm, lefts.at[pl.ds(0, span)], in_s.at[0]),
+        pltpu.make_async_copy(ul_hbm, lefts.at[pl.ds(span, span)], in_s.at[1]),
+        pltpu.make_async_copy(bg_hbm, bgu.at[:, pl.ds(0, cols)], in_s.at[2]),
+        pltpu.make_async_copy(bu_hbm, bgu.at[:, pl.ds(cols, cols)], in_s.at[3]),
+        pltpu.make_async_copy(bd_hbm, bd, in_s.at[4]),
+        pltpu.make_async_copy(dr_hbm, dr, in_s.at[5]),
+    ]
+    for load in loads:
+        load.start()
     pair = n + 1 - 2 * lax.rem(n, 2)
     across = lax.rem(n + 2, count)
     root = n == w
@@ -62,10 +76,19 @@
     for d in range(1, count):
         tok_copy(d).start()
 
+    named, ids = routes[...], jnp.zeros(routes.shape, jnp.int32)
+    for e in range(delta.shape[0]):
+        ids = jnp.where(named == e, delta[e], ids)
+    lanes = lax.broadcasted_iota(jnp.int32, wt.shape, 1)
+    table = jnp.zeros(wt.shape, f32)
+    for k in range(routes.shape[1]):
+        table = table + jnp.where(lanes == ids[:, k : k + 1], shares[:, k : k + 1], 0.0)
+    wt[...] = table
+    for load in loads[:4]:
+        load.wait()
+
     def low(rows, b):
-        for e in range(exp_here):
-            apart[b, :, e * rank : (e + 1) * rank] = dot32(rows, gl[e])
-            apart[b, :, span + e * rank : span + (e + 1) * rank] = dot32(rows, ul[e])
+        apart[b] = dot32t(rows, lefts[...])
 
     for d in range(count):
         b = up_of(count - d)
@@ -90,15 +113,13 @@
             pair_copy(d, xw.at[b]).start()
 
         rows = xw[b]
-        gate, up = dot32(rows, bg[...]), dot32(rows, bu[...])
+        both = dot32(rows, bgu[...])
         if d == 0:
-            gown[:, :cols] = gate
-            gown[:, cols:] = up
+            gown[...] = both
             for k in range(1, count):
                 wt_copy(k).start()
         else:
-            gsend[b, :, :cols] = gate.astype(bf16)
-            gsend[b, :, cols:] = up.astype(bf16)
+            gsend[b] = both.astype(bf16)
             copy(gsend.at[b], grecv.at[w], g_s.at[d], g_r.at[d], "wide", b).start()
 
     def a_copy(k):
@@ -126,6 +147,9 @@
 
     a_copy(1).wait_recv()
     afin[...] = (apart[...] + arecv[1].astype(f32)).astype(bf16)
+
+    def h_copy(slot, block, d, target):
+        return copy(hsend.at[block], hrecv.at[slot, block], h_s.at[d], h_r.at[slot, block], "wide", target)
 
     for d in range(count):
         b = up_of(count - d)
@@ -146,16 +170,13 @@
             up = ups + dot32(thin_rows[:, span + e * rank : span + (e + 1) * rank], ur[e])
             hidden = gate / (1.0 + jnp.exp(-gate)) * up * scale
             acc = hidden if acc is None else acc + hidden
-            bpart[b, :, e * rank : (e + 1) * rank] = dot32(hidden.astype(bf16), dl[e])
+            bpart[b, :, e * rank : (e + 1) * rank] = dot32t(hidden.astype(bf16), dl[e])
         hacc[b] = acc
         hsend[b] = acc.astype(bf16)
 
-    def h_copy(slot, target):
-        return copy(hsend, hrecv.at[slot], h_s, h_r.at[slot], "wide", target)
-
-    @pl.when(jnp.logical_not(root))
-    def _():
-        h_copy(w, n).start()
+        @pl.when(jnp.logical_not(root))
+        def _():
+            h_copy(w, b, d, n).start()
 
     def b_copy(k):
         return copy(bsend.at[k], brecv.at[k], b_s.at[k], b_r.at[k], "narrow", (pair, across)[k])
@@ -169,33 +190,39 @@
     b_copy(1).wait_recv()
     bfin[...] = (bpart[...] + brecv[1].astype(f32)).astype(bf16)
 
-    def hpair():
-        return copy(hpl, hpl, hb_s.at[0], hb_r, "narrow", pair)
-
-    def hacross():
-        return copy(hpl, hpl, hb_s.at[1], hb_r, "narrow", across)
-
-    @pl.when(root)
-    def _():
-        whole = hacc[...]
-        for d in range(1, count):
-            s = up_of(d)
-            h_copy(s, s).wait_recv()
-            whole = whole + hrecv[s].astype(f32)
-        hpl[...] = whole.astype(bf16)
-        hacross().start()
-        hpair().start()
-
-    @pl.when(jnp.logical_not(root))
-    def _():
-        hpair().wait_recv()
-
-    @pl.when(relay)
-    def _():
-        hpair().start()
+    def hpair(d):
+        b = up_of(count - d)
+        return copy(hpl.at[b], hpl.at[b], hb_s.at[0, d], hb_r.at[d], "narrow", pair)
+
+    def hacross(d):
+        b = up_of(count - d)
+        return copy(hpl.at[b], hpl.at[b], hb_s.at[1, d], hb_r.at[d], "narrow", across)
+
+    for load in loads[4:]:
+        load.wait()
 
     for d in (2, 1, 3, 0):
         b = up_of(count - d)
+
+        @pl.when(root)
+        def _():
+            whole = hacc[b]
+            for k in range(1, count):
+                src = up_of(k)
+                h_copy(src, b, d, src).wait_recv()
+                whole = whole + hrecv[src, b].astype(f32)
+            hpl[b] = whole.astype(bf16)
+            hacross(d).start()
+            hpair(d).start()
+
+        @pl.when(jnp.logical_not(root))
+        def _():
+            hpair(d).wait_recv()
+
+        @pl.when(relay)
+        def _():
+            hpair(d).start()
+
         part = dot32(hpl[b], bd[...]) + dot32(bfin[b], dr[...])
         if d == 0:
             oown[...] = part
@@ -226,38 +253,47 @@
             src = tok if d == 0 else xcol.at[up_of(count - d)]
             across_copy(d, src).wait_send()
             pair_copy(d, src).wait_send()
-        hacross().wait_send()
-        hpair().wait_send()
+            hacross(d).wait_send()
+            hpair(d).wait_send()
 
     @pl.when(relay)
     def _():
         for d in range(count):
             pair_copy(d, xw.at[up_of(count - d)]).wait_send()
-        hpair().wait_send()
+            hpair(d).wait_send()
 
     @pl.when(jnp.logical_not(root))
     def _():
-        h_copy(w, n).wait_send()
-
-
-def fused(tokens, weight_of, bg, bu, bd, gl, gr, ul, ur, dl, dr):
+        for d in range(count):
+            h_copy(w, up_of(count - d), d, n).wait_send()
+
+
+def fused(tokens, routes, shares, delta, bg, bu, bd, gl, gr, ul, ur, dl, dr):
     bf16, f32 = jnp.bfloat16, jnp.float32
     count = PLANE
     rows, feats = tokens.shape
-    cols = bg.shape[1]
-    exp_here, rank = gl.shape[0], gl.shape[2]
+    depth, cols = bg.shape
+    exp_here, rank, _ = gr.shape
     span = exp_here * rank
-    lanes = -(-weight_of.shape[1] // 128) * 128
-    wt = jnp.pad(weight_of, ((0, 0), (0, lanes - weight_of.shape[1])))
+    lanes = -(-delta.shape[0] // 128) * 128
     sem = pltpu.SemaphoreType.DMA
     vm = pltpu.VMEM
     out_feats = bd.shape[1]
+    vmem, hbm = pl.BlockSpec(memory_space=pltpu.VMEM), pl.BlockSpec(memory_space=pl.ANY)
     return pl.pallas_call(
         kernel,
         out_shape=jax.ShapeDtypeStruct((rows, out_feats), bf16),
-        in_specs=[pl.BlockSpec(memory_space=pltpu.VMEM)] * 11,
+        in_specs=[
+            vmem, vmem, vmem, pl.BlockSpec(memory_space=pltpu.SMEM),
+            hbm, hbm, hbm, hbm, vmem, hbm, vmem, vmem, hbm,
+        ],
         out_specs=pl.BlockSpec(memory_space=pltpu.VMEM),
         scratch_shapes=[
+            vm((rows, lanes), f32),
+            vm((depth, 2 * cols), bf16),
+            vm((2 * span, feats), bf16),
+            vm(bd.shape, bf16),
+            vm((span, out_feats), bf16),
             vm((count, rows, feats), bf16),
             vm((count, rows, feats), bf16),
             vm((count, rows, lanes), f32),
@@ -285,11 +321,16 @@
             sem((count, 2)), sem((count,)),
             sem((count,)), sem((count,)), sem((count,)), sem((count,)),
             sem((2,)), sem((2,)),
-            sem, sem((count,)), sem((2,)), sem,
-            sem((2,)), sem((2,)), sem((count,)), sem((count,)),
+            sem((count,)), sem((count, count)), sem((2, count)), sem((count,)),
+            sem((2,)), sem((2,)), sem((count,)), sem((count,)), sem((6,)),
         ],
         compiler_params=pltpu.CompilerParams(collective_id=0, has_side_effects=True, vmem_limit_bytes=60 * 1024 * 1024),
-    )(tokens, wt, bg, bu, bd, gl, gr, ul, ur, dl, dr.reshape(span, out_feats))
+    )(
+        tokens, routes, shares, delta, bg, bu, bd,
+        jnp.swapaxes(gl, 1, 2).reshape(span, feats), gr,
+        jnp.swapaxes(ul, 1, 2).reshape(span, feats), ur,
+        jnp.swapaxes(dl, 1, 2), dr.reshape(span, out_feats),
+    )
 
 
 def shards(
@@ -307,6 +348,11 @@
     down_left,
     down_right,
 ):
+    if lax.axis_size("narrow") == PLANE and lax.axis_size("wide") == PLANE:
+        return fused(
+            tokens, routes, gate_weights, delta_of, base_gate, base_up, base_down,
+            gate_left, gate_right, up_left, up_right, down_left, down_right,
+        )
     exp_here, _, rank = gate_left.shape
     experts = delta_of.shape[0]
     mine = lax.axis_index("wide")
@@ -318,8 +364,6 @@
     weight_of = jnp.sum(
         jnp.where(delta_ids[:, :, None] == expert_ids, gate_weights[:, :, None], 0.0), axis=1
     )
-    if lax.axis_size("narrow") == PLANE and lax.axis_size("wide") == PLANE:
-        return fused(tokens, weight_of, base_gate, base_up, base_down, gate_left, gate_right, up_left, up_right, down_left, down_right)
     weights = lax.all_gather(weight_of, "wide", axis=0, tiled=True)
     weights = lax.dynamic_slice_in_dim(weights, mine * exp_here, exp_here, axis=1)
 

time: 75.8 us -> 68.1 us (0.90)
  Pallas kernels: 67.5 us -> 63.6 us
  local copies, waits for them, and re-layouts: 5.95 us -> 3.65 us
  other arithmetic: 1.53 us -> 0 us
    pallas_call x1, Pallas kernels: 67.5 us -> 63.6 us  [fused(): pl.pallas_call(kernel, out_shape=jax.ShapeDtypeStruct((rows, out_feats),...]
    unnamed x10 -> x7, local copies, waits for them, and re-layouts: 5.24 us -> 3.65 us
    reduce_sum x2 -> x0, other arithmetic: 1.53 us -> none  [the longest x1 0.82 us: shards(): delta_ids = jnp.sum(jnp.where(named, delta_of[None, None, :], 0), axis=2)]
where the time goes in v3:
time: 68.1 us; the launch traced here: 67.2 us
  Pallas kernels  63.6 us (93%)
  local copies, waits for them, and re-layouts  3.65 us (5%)
    pallas_call x1, Pallas kernels, fused(): pl.pallas_call(kernel, out_shape=jax.ShapeDtypeStruct((rows, out_feats),...  63.6 us
    unnamed x7, local copies, waits for them, and re-layouts  3.65 us

profile of v3, /device:TPU:0, one launch (start us, length us, event | category | flops | bytes accessed | tf_op | source)
XLA Modules:
  0.0 67.2 jit_solution(7968117433595465665)
XLA Ops:
  0.0 0.0 copy-start
  0.0 0.7 %copy-done = s32[64,8]{0,1:T(8,128)S(1)} copy-done((s32[64,8]{0,1:T(8,128)S(1)}, s32[64,8]{0,1:T(8,128)}, u32[]{:S(2)}) %copy-start) | copy-done | bytes 2072
  0.7 0.0 copy-start.1
  0.7 0.7 %copy.14.routes = s32[64,8]{1,0:T(8,128)} copy(s32[64,8]{0,1:T(8,128)S(1)} %copy-done) | data formatting | bytes 4096 | tf_op args[1]
  1.4 0.0 copy-done.1
  1.4 0.7 %copy.15.shares = f32[64,8]{1,0:T(8,128)} copy(f32[64,8]{0,1:T(8,128)S(1)} %copy-done.1) | data formatting | bytes 4096 | tf_op args[2]
  2.1 63.6 %shard_map.127 = bf16[64,1024]{1,0:T(8,128)(2,1)} custom-call(bf16[64,1024]{1,0:T(8,128)(2,1)} %tok.1, s32[64,8]{1,0:T(8,128)} %copy.14.routes, f32[64,8]{1,0:T(8,128)} %copy.15.shares, s32[16]{0:T(128)} %delta.1, bf16[1024,384]{1,0:T(8,128)(2,1)} %bg_hbm.1, bf16[1024,384]{1,0:T(8,128)(2,1)} %bu_hbm.1, bf16[384,1024]{1,0:T(8,128)(2,1)} %bd_hbm.1, ...), custom_call_target="tpu_custom_call" | custom-call | tf_op jit(solution)/shard_map/pallas_call | solution.py:283
  65.7 1.6 %copy.17 = bf16[64,1024]{1,0:T(8,128)(2,1)} copy(bf16[64,1024]{1,0:T(8,128)(2,1)} %shard_map.127) | data formatting | bytes 262144
Async XLA Ops:
  0.0 0.7 %copy-start = (s32[64,8]{0,1:T(8,128)S(1)}, s32[64,8]{0,1:T(8,128)}, u32[]{:S(2)}) copy-start(s32[64,8]{0,1:T(8,128)} %param.14) | copy-start | bytes 6148
  0.7 0.7 %copy-start.1 = (f32[64,8]{0,1:T(8,128)S(1)}, f32[64,8]{0,1:T(8,128)}, u32[]{:S(2)}) copy-start(f32[64,8]{0,1:T(8,128)} %param.15) | copy-start | bytes 6148

commit v4 on v3

--- a/solution.py
+++ b/solution.py
@@ -15,6 +15,8 @@
 
 
 PLANE = 4
+
+LANES = 128
 
 
 def kernel(
@@ -33,11 +35,15 @@
     loads = [
         pltpu.make_async_copy(gl_hbm, lefts.at[pl.ds(0, span)], in_s.at[0]),
         pltpu.make_async_copy(ul_hbm, lefts.at[pl.ds(span, span)], in_s.at[1]),
-        pltpu.make_async_copy(bg_hbm, bgu.at[:, pl.ds(0, cols)], in_s.at[2]),
-        pltpu.make_async_copy(bu_hbm, bgu.at[:, pl.ds(cols, cols)], in_s.at[3]),
-        pltpu.make_async_copy(bd_hbm, bd, in_s.at[4]),
-        pltpu.make_async_copy(dr_hbm, dr, in_s.at[5]),
     ]
+    chunk = LANES if cols % LANES == 0 else cols
+    chunks = cols // chunk
+    for c in range(chunks):
+        for k, base in enumerate((bg_hbm, bu_hbm)):
+            place = bgu.at[:, pl.ds((2 * c + k) * chunk, chunk)]
+            loads.append(pltpu.make_async_copy(base.at[:, pl.ds(c * chunk, chunk)], place, in_s.at[2 + 2 * c + k]))
+    loads.append(pltpu.make_async_copy(bd_hbm, bd, in_s.at[2 + 2 * chunks]))
+    loads.append(pltpu.make_async_copy(dr_hbm, dr, in_s.at[3 + 2 * chunks]))
     for load in loads:
         load.start()
     pair = n + 1 - 2 * lax.rem(n, 2)
@@ -76,15 +82,19 @@
     for d in range(1, count):
         tok_copy(d).start()
 
+    def g_copy(d, c, peer, slot):
+        part = pl.ds(2 * c * chunk, 2 * chunk)
+        return copy(gsend.at[peer, :, part], grecv.at[slot, :, part], g_s.at[d, c], g_r.at[d, c], "wide", peer)
+
     named, ids = routes[...], jnp.zeros(routes.shape, jnp.int32)
     for e in range(delta.shape[0]):
         ids = jnp.where(named == e, delta[e], ids)
-    lanes = lax.broadcasted_iota(jnp.int32, wt.shape, 1)
-    table = jnp.zeros(wt.shape, f32)
-    for k in range(routes.shape[1]):
-        table = table + jnp.where(lanes == ids[:, k : k + 1], shares[:, k : k + 1], 0.0)
-    wt[...] = table
-    for load in loads[:4]:
+    sets = lax.broadcasted_iota(jnp.int32, (wt.shape[1], wt.shape[0]), 0)
+    table = jnp.zeros(sets.shape, f32)
+    for k in range(routes.shape[0]):
+        table = table + jnp.where(sets == ids[k : k + 1], shares[k : k + 1, :], 0.0)
+    wt[...] = table.T
+    for load in loads[:-2]:
         load.wait()
 
     def low(rows, b):
@@ -120,7 +130,8 @@
                 wt_copy(k).start()
         else:
             gsend[b] = both.astype(bf16)
-            copy(gsend.at[b], grecv.at[w], g_s.at[d], g_r.at[d], "wide", b).start()
+            for c in range(chunks):
+                g_copy(d, c, b, w).start()
 
     def a_copy(k):
         return copy(asend.at[k], arecv.at[k], a_s.at[k], a_r.at[k], "narrow", (pair, across)[k])
@@ -132,51 +143,61 @@
     asend[1] = apart[...].astype(bf16)
     a_copy(1).start()
 
-    def ga_copy(d):
-        return copy(gred, gall.at[w], ga_s.at[d], ga_r.at[d], "wide", up_of(d))
-
-    total = gown[...]
-    for d in range(1, count):
-        s = up_of(d)
-        copy(gsend.at[s], grecv.at[s], g_s.at[d], g_r.at[d], "wide", s).wait_recv()
-        total = total + grecv[s].astype(f32)
-    gown[...] = total
-    gred[...] = total.astype(bf16)
-    for d in range(1, count):
-        ga_copy(d).start()
+    def ga_copy(d, c):
+        part = pl.ds(2 * c * chunk, 2 * chunk)
+        return copy(gred.at[:, part], gall.at[w, :, part], ga_s.at[d, c], ga_r.at[d, c], "wide", up_of(d))
+
+    for c in range(chunks):
+        part = slice(2 * c * chunk, 2 * (c + 1) * chunk)
+        total = gown[:, part]
+        for d in range(1, count):
+            g_copy(d, c, up_of(d), up_of(d)).wait_recv()
+            total = total + grecv[up_of(d), :, part].astype(f32)
+        gown[:, part] = total
+        gred[:, part] = total.astype(bf16)
+        for d in range(1, count):
+            ga_copy(d, c).start()
 
     a_copy(1).wait_recv()
     afin[...] = (apart[...] + arecv[1].astype(f32)).astype(bf16)
 
-    def h_copy(slot, block, d, target):
-        return copy(hsend.at[block], hrecv.at[slot, block], h_s.at[d], h_r.at[slot, block], "wide", target)
-
-    for d in range(count):
-        b = up_of(count - d)
-        if d > 0:
-            ga_copy(d).wait_recv()
-            wt_copy(d).wait_recv()
-            gates, ups = gall[b, :, :cols].astype(f32), gall[b, :, cols:].astype(f32)
-            scales = wts[b]
-        else:
-            gates, ups = gown[:, :cols], gown[:, cols:]
-            scales = wt[...]
-        ids = lax.broadcasted_iota(jnp.int32, scales.shape, 1)
-        thin_rows = afin[b]
-        acc = None
-        for e in range(exp_here):
-            scale = jnp.sum(jnp.where(ids == w * exp_here + e, scales, 0.0), axis=1, keepdims=True)
-            gate = gates + dot32(thin_rows[:, e * rank : (e + 1) * rank], gr[e])
-            up = ups + dot32(thin_rows[:, span + e * rank : span + (e + 1) * rank], ur[e])
-            hidden = gate / (1.0 + jnp.exp(-gate)) * up * scale
-            acc = hidden if acc is None else acc + hidden
-            bpart[b, :, e * rank : (e + 1) * rank] = dot32t(hidden.astype(bf16), dl[e])
-        hacc[b] = acc
-        hsend[b] = acc.astype(bf16)
+    def h_copy(slot, c, target):
+        part = pl.ds(c * chunk, chunk)
+        return copy(hsend.at[:, :, part], hrecv.at[slot, :, :, part], h_s.at[c], h_r.at[slot, c], "wide", target)
+
+    for c in range(chunks):
+        gate_part = slice(2 * c * chunk, (2 * c + 1) * chunk)
+        up_part = slice((2 * c + 1) * chunk, 2 * (c + 1) * chunk)
+        part = slice(c * chunk, (c + 1) * chunk)
+        for d in range(count):
+            b = up_of(count - d)
+            if d > 0:
+                ga_copy(d, c).wait_recv()
+                if c == 0:
+                    wt_copy(d).wait_recv()
+                gates, ups = gall[b, :, gate_part].astype(f32), gall[b, :, up_part].astype(f32)
+                scales = wts[b]
+            else:
+                gates, ups = gown[:, gate_part], gown[:, up_part]
+                scales = wt[...]
+            ids = lax.broadcasted_iota(jnp.int32, scales.shape, 1)
+            thin_rows = afin[b]
+            acc = None
+            for e in range(exp_here):
+                scale = jnp.sum(jnp.where(ids == w * exp_here + e, scales, 0.0), axis=1, keepdims=True)
+                own = slice(e * rank, (e + 1) * rank)
+                gate = gates + dot32(thin_rows[:, own], gr[e, :, part])
+                up = ups + dot32(thin_rows[:, span + e * rank : span + (e + 1) * rank], ur[e, :, part])
+                hidden = gate / (1.0 + jnp.exp(-gate)) * up * scale
+                acc = hidden if acc is None else acc + hidden
+                thin = dot32t(hidden.astype(bf16), dl[e, :, part])
+                bpart[b, :, own] = thin if c == 0 else bpart[b, :, own] + thin
+            hacc[b, :, part] = acc
+            hsend[b, :, part] = acc.astype(bf16)
 
         @pl.when(jnp.logical_not(root))
         def _():
-            h_copy(w, b, d, n).start()
+            h_copy(w, c, n).start()
 
     def b_copy(k):
         return copy(bsend.at[k], brecv.at[k], b_s.at[k], b_r.at[k], "narrow", (pair, across)[k])
@@ -198,7 +219,7 @@
         b = up_of(count - d)
         return copy(hpl.at[b], hpl.at[b], hb_s.at[1, d], hb_r.at[d], "narrow", across)
 
-    for load in loads[4:]:
+    for load in loads[-2:]:
         load.wait()
 
     for d in (2, 1, 3, 0):
@@ -209,7 +230,9 @@
             whole = hacc[b]
             for k in range(1, count):
                 src = up_of(k)
-                h_copy(src, b, d, src).wait_recv()
+                if d == 2:
+                    for c in range(chunks):
+                        h_copy(src, c, src).wait_recv()
                 whole = whole + hrecv[src, b].astype(f32)
             hpl[b] = whole.astype(bf16)
             hacross(d).start()
@@ -240,8 +263,9 @@
         b = up_of(count - d)
         tok_copy(d).wait_send()
         wt_copy(d).wait_send()
-        ga_copy(d).wait_send()
-        copy(gsend.at[b], grecv.at[w], g_s.at[d], g_r.at[d], "wide", b).wait_send()
+        for c in range(chunks):
+            ga_copy(d, c).wait_send()
+            g_copy(d, c, b, w).wait_send()
         copy(osend.at[b], orecv.at[w], o_s.at[d], o_r.at[d], "wide", b).wait_send()
     for k in range(2):
         a_copy(k).wait_send()
@@ -264,8 +288,8 @@
 
     @pl.when(jnp.logical_not(root))
     def _():
-        for d in range(count):
-            h_copy(w, up_of(count - d), d, n).wait_send()
+        for c in range(chunks):
+            h_copy(w, c, n).wait_send()
 
 
 def fused(tokens, routes, shares, delta, bg, bu, bd, gl, gr, ul, ur, dl, dr):
@@ -275,7 +299,8 @@
     depth, cols = bg.shape
     exp_here, rank, _ = gr.shape
     span = exp_here * rank
-    lanes = -(-delta.shape[0] // 128) * 128
+    lanes = -(-delta.shape[0] // LANES) * LANES
+    chunks = cols // LANES if cols % LANES == 0 else 1
     sem = pltpu.SemaphoreType.DMA
     vm = pltpu.VMEM
     out_feats = bd.shape[1]
@@ -319,14 +344,14 @@
             vm((rows, out_feats), f32),
             sem((count,)), sem((count,)), sem((count,)), sem((count,)),
             sem((count, 2)), sem((count,)),
-            sem((count,)), sem((count,)), sem((count,)), sem((count,)),
+            sem((count, chunks)), sem((count, chunks)), sem((count, chunks)), sem((count, chunks)),
             sem((2,)), sem((2,)),
-            sem((count,)), sem((count, count)), sem((2, count)), sem((count,)),
-            sem((2,)), sem((2,)), sem((count,)), sem((count,)), sem((6,)),
+            sem((chunks,)), sem((count, chunks)), sem((2, count)), sem((count,)),
+            sem((2,)), sem((2,)), sem((count,)), sem((count,)), sem((4 + 2 * chunks,)),
         ],
         compiler_params=pltpu.CompilerParams(collective_id=0, has_side_effects=True, vmem_limit_bytes=60 * 1024 * 1024),
     )(
-        tokens, routes, shares, delta, bg, bu, bd,
+        tokens, routes.T, shares.T, delta, bg, bu, bd,
         jnp.swapaxes(gl, 1, 2).reshape(span, feats), gr,
         jnp.swapaxes(ul, 1, 2).reshape(span, feats), ur,
         jnp.swapaxes(dl, 1, 2), dr.reshape(span, out_feats),

time: 68.1 us -> 65 us (0.954)
  local copies, waits for them, and re-layouts: 3.65 us -> 1.57 us
  Pallas kernels: 63.6 us -> 62.6 us
    unnamed x7 -> x1, local copies, waits for them, and re-layouts: 3.65 us -> 1.57 us
    pallas_call x1, Pallas kernels: 63.6 us -> 62.6 us  [fused(): pl.pallas_call(kernel, out_shape=jax.ShapeDtypeStruct((rows, out_feats),...]
where the time goes in v4:
time: 65 us; the launch traced here: 64.2 us
  Pallas kernels  62.6 us (96%)
  local copies, waits for them, and re-layouts  1.57 us (2%)
    pallas_call x1, Pallas kernels, fused(): pl.pallas_call(kernel, out_shape=jax.ShapeDtypeStruct((rows, out_feats),...  62.6 us
    unnamed x1, local copies, waits for them, and re-layouts  1.57 us

profile of v4, /device:TPU:0, one launch (start us, length us, event | category | flops | bytes accessed | tf_op | source)
XLA Modules:
  0.0 64.2 jit_solution(18235098198761163896)
XLA Ops:
  0.0 62.6 %shard_map.127 = bf16[64,1024]{1,0:T(8,128)(2,1)} custom-call(bf16[64,1024]{1,0:T(8,128)(2,1)} %tok.1, s32[8,64]{1,0:T(8,128)} %bitcast.14, f32[8,64]{1,0:T(8,128)} %bitcast.15, s32[16]{0:T(128)} %delta.1, bf16[1024,384]{1,0:T(8,128)(2,1)} %bg_hbm.1, bf16[1024,384]{1,0:T(8,128)(2,1)} %bu_hbm.1, bf16[384,1024]{1,0:T(8,128)(2,1)} %bd_hbm.1, ...), custom_call_target="tpu_custom_call" | custom-call | tf_op jit(solution)/shard_map/pallas_call | solution.py:308
  62.6 1.6 %copy.15 = bf16[64,1024]{1,0:T(8,128)(2,1)} copy(bf16[64,1024]{1,0:T(8,128)(2,1)} %shard_map.127) | data formatting | bytes 262144

commit v5 on v4

--- a/solution.py
+++ b/solution.py
@@ -1,3 +1,5 @@
+import functools
+
 import jax
 import jax.numpy as jnp
 from jax import lax
@@ -67,20 +69,37 @@
         pl.semaphore_signal(barrier, inc=1, device_id={"narrow": peer}, device_id_type=pl.DeviceIdType.MESH)
     pl.semaphore_wait(barrier, count + 1)
 
-    def tok_copy(d):
-        return copy(tok, xcol.at[w], tok_s.at[d], tok_r.at[d], "wide", up_of(d))
+    def tok_copy(way, hop):
+        peer = up_of((1, count - 1)[way])
+        block = up_of((count - hop + 1, hop - 1)[way])
+        src = tok if hop == 1 else xcol.at[block]
+        return copy(src, xcol.at[block], tok_s.at[way, hop], tok_r.at[way, hop], "wide", peer)
+
+    def open_way(way):
+        return (w < count - 1, w > 0)[way]
+
+    def reaches(way, hop):
+        return (w >= hop, w + hop < count)[way]
+
+    visits = [(0, 0, None)] + [(hop, way, reaches(way, hop)) for hop in range(1, count) for way in range(2)]
+
+    def block_of(hop, way):
+        return up_of(((count - hop) % count, hop)[way])
 
     def wt_copy(d):
         return copy(wt, wts.at[w], wt_s.at[d], wt_r.at[d], "wide", up_of(d))
 
-    def pair_copy(d, src):
-        return copy(src, xw.at[up_of(count - d)], bs_s.at[d, 0], bs_r.at[d], "narrow", pair)
-
-    def across_copy(d, src):
-        return copy(src, xw.at[up_of(count - d)], bs_s.at[d, 1], bs_r.at[d], "narrow", across)
-
-    for d in range(1, count):
-        tok_copy(d).start()
+    def pair_copy(b, src):
+        return copy(src, xw.at[b], bs_s.at[b, 0], bs_r.at[b], "narrow", pair)
+
+    def across_copy(b, src):
+        return copy(src, xw.at[b], bs_s.at[b, 1], bs_r.at[b], "narrow", across)
+
+    for way in range(2):
+
+        @pl.when(open_way(way))
+        def _():
+            tok_copy(way, 1).start()
 
     def g_copy(d, c, peer, slot):
         part = pl.ds(2 * c * chunk, 2 * chunk)
@@ -100,38 +119,48 @@
     def low(rows, b):
         apart[b] = dot32t(rows, lefts[...])
 
-    for d in range(count):
-        b = up_of(count - d)
-        if d > 0:
-            tok_copy(d).wait_recv()
-        mine = tok if d == 0 else xcol.at[b]
+    def visit(hop, way):
+        b = block_of(hop, way)
+        mine = tok if hop == 0 else xcol.at[b]
+        if hop > 0:
+            tok_copy(way, hop).wait_recv()
+        if 0 < hop < count - 1:
+
+            @pl.when(open_way(way))
+            def _():
+                tok_copy(way, hop + 1).start()
 
         @pl.when(root)
         def _():
-            across_copy(d, mine).start()
-            pair_copy(d, mine).start()
+            across_copy(b, mine).start()
+            pair_copy(b, mine).start()
             xw[b] = mine[...]
 
         low(mine[...], b)
 
         @pl.when(jnp.logical_not(root))
         def _():
-            pair_copy(d, xw.at[b]).wait_recv()
+            pair_copy(b, xw.at[b]).wait_recv()
 
         @pl.when(relay)
         def _():
-            pair_copy(d, xw.at[b]).start()
-
-        rows = xw[b]
-        both = dot32(rows, bgu[...])
-        if d == 0:
+            pair_copy(b, xw.at[b]).start()
+
+        both = dot32(xw[b], bgu[...])
+        if hop == 0:
             gown[...] = both
             for k in range(1, count):
                 wt_copy(k).start()
         else:
             gsend[b] = both.astype(bf16)
             for c in range(chunks):
-                g_copy(d, c, b, w).start()
+                g_copy((hop, count - hop)[way], c, b, w).start()
+
+    for hop, way, there in visits:
+        if there is None:
+            visit(hop, way)
+        else:
+            pl.when(there)(functools.partial(visit, hop, way))
 
     def a_copy(k):
         return copy(asend.at[k], arecv.at[k], a_s.at[k], a_r.at[k], "narrow", (pair, across)[k])
@@ -261,12 +290,23 @@
 
     for d in range(1, count):
         b = up_of(count - d)
-        tok_copy(d).wait_send()
         wt_copy(d).wait_send()
         for c in range(chunks):
             ga_copy(d, c).wait_send()
             g_copy(d, c, b, w).wait_send()
         copy(osend.at[b], orecv.at[w], o_s.at[d], o_r.at[d], "wide", b).wait_send()
+    for way in range(2):
+
+        @pl.when(open_way(way))
+        def _():
+            tok_copy(way, 1).wait_send()
+
+        for hop in range(1, count - 1):
+
+            @pl.when(jnp.logical_and(open_way(way), reaches(way, hop)))
+            def _():
+                tok_copy(way, hop + 1).wait_send()
+
     for k in range(2):
         a_copy(k).wait_send()
         b_copy(k).wait_send()
@@ -274,16 +314,18 @@
     @pl.when(root)
     def _():
         for d in range(count):
-            src = tok if d == 0 else xcol.at[up_of(count - d)]
-            across_copy(d, src).wait_send()
-            pair_copy(d, src).wait_send()
+            b = up_of(count - d)
+            src = tok if d == 0 else xcol.at[b]
+            across_copy(b, src).wait_send()
+            pair_copy(b, src).wait_send()
             hacross(d).wait_send()
             hpair(d).wait_send()
 
     @pl.when(relay)
     def _():
         for d in range(count):
-            pair_copy(d, xw.at[up_of(count - d)]).wait_send()
+            b = up_of(count - d)
+            pair_copy(b, xw.at[b]).wait_send()
             hpair(d).wait_send()
 
     @pl.when(jnp.logical_not(root))
@@ -342,7 +384,7 @@
             vm((count, rows, out_feats), bf16),
             vm((count, rows, out_feats), bf16),
             vm((rows, out_feats), f32),
-            sem((count,)), sem((count,)), sem((count,)), sem((count,)),
+            sem((2, count)), sem((2, count)), sem((count,)), sem((count,)),
             sem((count, 2)), sem((count,)),
             sem((count, chunks)), sem((count, chunks)), sem((count, chunks)), sem((count, chunks)),
             sem((2,)), sem((2,)),

time: 65 us -> 77.1 us (1.19)
  Pallas kernels: 62.6 us -> 74.8 us
    pallas_call x1, Pallas kernels: 62.6 us -> 74.8 us  [fused(): pl.pallas_call(kernel, out_shape=jax.ShapeDtypeStruct((rows, out_feats),...]
where the time goes in v5:
time: 77.1 us; the launch traced here: 76.3 us
  Pallas kernels  74.8 us (97%)
  local copies, waits for them, and re-layouts  1.57 us (2%)
    pallas_call x1, Pallas kernels, fused(): pl.pallas_call(kernel, out_shape=jax.ShapeDtypeStruct((rows, out_feats),...  74.8 us
    unnamed x1, local copies, waits for them, and re-layouts  1.57 us

profile of v5, /device:TPU:0, one launch (start us, length us, event | category | flops | bytes accessed | tf_op | source)
XLA Modules:
  0.0 76.3 jit_solution(222276656201764075)
XLA Ops:
  0.0 74.8 %shard_map.127 = bf16[64,1024]{1,0:T(8,128)(2,1)} custom-call(bf16[64,1024]{1,0:T(8,128)(2,1)} %tok.1, s32[8,64]{1,0:T(8,128)} %bitcast.14, f32[8,64]{1,0:T(8,128)} %bitcast.15, s32[16]{0:T(128)} %delta.1, bf16[1024,384]{1,0:T(8,128)(2,1)} %bg_hbm.1, bf16[1024,384]{1,0:T(8,128)(2,1)} %bu_hbm.1, bf16[384,1024]{1,0:T(8,128)(2,1)} %bd_hbm.1, ...), custom_call_target="tpu_custom_call" | custom-call | tf_op jit(solution)/shard_map/pallas_call | solution.py:350
  74.8 1.6 %copy.15 = bf16[64,1024]{1,0:T(8,128)(2,1)} copy(bf16[64,1024]{1,0:T(8,128)(2,1)} %shard_map.127) | data formatting | bytes 262144

commit v6 on v4

--- a/solution.py
+++ b/solution.py
@@ -89,11 +89,11 @@
     named, ids = routes[...], jnp.zeros(routes.shape, jnp.int32)
     for e in range(delta.shape[0]):
         ids = jnp.where(named == e, delta[e], ids)
-    sets = lax.broadcasted_iota(jnp.int32, (wt.shape[1], wt.shape[0]), 0)
+    sets = lax.broadcasted_iota(jnp.int32, wt.shape, 0)
     table = jnp.zeros(sets.shape, f32)
     for k in range(routes.shape[0]):
         table = table + jnp.where(sets == ids[k : k + 1], shares[k : k + 1, :], 0.0)
-    wt[...] = table.T
+    wt[...] = table
     for load in loads[:-2]:
         load.wait()
 
@@ -176,10 +176,10 @@
                 if c == 0:
                     wt_copy(d).wait_recv()
                 gates, ups = gall[b, :, gate_part].astype(f32), gall[b, :, up_part].astype(f32)
-                scales = wts[b]
+                scales = wts[b].T
             else:
                 gates, ups = gown[:, gate_part], gown[:, up_part]
-                scales = wt[...]
+                scales = wt[...].T
             ids = lax.broadcasted_iota(jnp.int32, scales.shape, 1)
             thin_rows = afin[b]
             acc = None
@@ -299,7 +299,6 @@
     depth, cols = bg.shape
     exp_here, rank, _ = gr.shape
     span = exp_here * rank
-    lanes = -(-delta.shape[0] // LANES) * LANES
     chunks = cols // LANES if cols % LANES == 0 else 1
     sem = pltpu.SemaphoreType.DMA
     vm = pltpu.VMEM
@@ -314,14 +313,14 @@
         ],
         out_specs=pl.BlockSpec(memory_space=pltpu.VMEM),
         scratch_shapes=[
-            vm((rows, lanes), f32),
+            vm((delta.shape[0], rows), f32),
             vm((depth, 2 * cols), bf16),
             vm((2 * span, feats), bf16),
             vm(bd.shape, bf16),
             vm((span, out_feats), bf16),
             vm((count, rows, feats), bf16),
             vm((count, rows, feats), bf16),
-            vm((count, rows, lanes), f32),
+            vm((count, delta.shape[0], rows), f32),
             vm((count, rows, 2 * cols), bf16),
             vm((count, rows, 2 * cols), bf16),
             vm((rows, 2 * cols), f32),

time: 65 us -> 66.2 us (1.018)
  Pallas kernels: 62.6 us -> 63.8 us
    pallas_call x1, Pallas kernels: 62.6 us -> 63.8 us  [fused(): pl.pallas_call(kernel, out_shape=jax.ShapeDtypeStruct((rows, out_feats),...]
where the time goes in v6:
time: 66.2 us; the launch traced here: 65.4 us
  Pallas kernels  63.8 us (96%)
  local copies, waits for them, and re-layouts  1.57 us (2%)
    pallas_call x1, Pallas kernels, fused(): pl.pallas_call(kernel, out_shape=jax.ShapeDtypeStruct((rows, out_feats),...  63.8 us
    unnamed x1, local copies, waits for them, and re-layouts  1.57 us

profile of v6, /device:TPU:0, one launch (start us, length us, event | category | flops | bytes accessed | tf_op | source)
XLA Modules:
  0.0 65.4 jit_solution(2571306096246589707)
XLA Ops:
  0.0 63.8 %shard_map.127 = bf16[64,1024]{1,0:T(8,128)(2,1)} custom-call(bf16[64,1024]{1,0:T(8,128)(2,1)} %tok.1, s32[8,64]{1,0:T(8,128)} %bitcast.14, f32[8,64]{1,0:T(8,128)} %bitcast.15, s32[16]{0:T(128)} %delta.1, bf16[1024,384]{1,0:T(8,128)(2,1)} %bg_hbm.1, bf16[1024,384]{1,0:T(8,128)(2,1)} %bu_hbm.1, bf16[384,1024]{1,0:T(8,128)(2,1)} %bd_hbm.1, ...), custom_call_target="tpu_custom_call" | custom-call | tf_op jit(solution)/shard_map/pallas_call | solution.py:307
  63.8 1.6 %copy.15 = bf16[64,1024]{1,0:T(8,128)(2,1)} copy(bf16[64,1024]{1,0:T(8,128)(2,1)} %shard_map.127) | data formatting | bytes 262144
